TPU v7x, 32 devices: a whole 2x2x4 slice. The times are simulated.
32 devices in a mesh: lat: 8 (over y, x, core), lon: 4 (over z).
Axes of the slice: x: 2, y: 2, z: 4, core: 2. Of those that a mesh axis runs over, the one named last changes fastest.
Arguments:
- adjoint_in: float32 [2, 24, 128, 2880], P(None, None, 'lat', 'lon'), may hold values from -6 to 6
- wind_east: float32 [24, 128, 2880], P(None, 'lat', 'lon'), may hold values from -0.45 to 0.45
- wind_north: float32 [24, 128, 2880], P(None, 'lat', 'lon'), may hold values from -0.45 to 0.45
- polar_mask: int32 [128], replicated, may hold values from 0 to 1, as said below
- obs_owner: int32 [131072, 1], P(('lat', 'lon')), may hold values from 0 to 31; in each aligned block of 4096 rows (0 to 4095, 4096 to 8191, ...) at most 256 rows name the same one
- obs_cell: int32 [131072], P(('lat', 'lon')), may hold values from 0 to 11519
- obs_kernel: float32 [131072, 24], P(('lat', 'lon')), may hold values from 0.2 to 2
- obs_resid: float32 [131072, 2], P(('lat', 'lon')), may hold values from -6 to 6
Outputs:
- adjoint_out: float32 [2, 24, 128, 2880], P(None, None, 'lat', 'lon')
Inputs may be any that keep to these rules, and one draw needn't show every extreme that they name: polar_mask is 1 exactly on the first KS rows and the last KN rows, with KS and KN each from 1 to 16 and one of them equal to 16. `obs_owner`: among the soundings of one device no owner is named more than 256 times, and in every draw some device names some owner exactly 256 times.
All inputs are finite; a program needn't handle non-finite values.
Results may differ from a plain program's by a relative error of at most 0.00008.
Values sent between devices are 32-bit elements; how exact they have to be, the bound alone decides.
A program may use at most 128 MiB of HBM per device.

v0:
```python
import math

import jax
import jax.numpy as jnp
from jax import lax
from jax.sharding import PartitionSpec as P

precise_mode = lax.Precision.HIGHEST


def with_halo(block, sides, width):
    for axis, dim in sides:
        count = lax.axis_size(axis)
        forward = [(i, i + 1) for i in range(count - 1)]
        forward.append((count - 1, 0))
        backward = [(target, source) for source, target in forward]
        low = lax.ppermute(
            lax.slice_in_dim(block, block.shape[dim] - width, None, axis=dim), axis, forward
        )
        high = lax.ppermute(lax.slice_in_dim(block, 0, width, axis=dim), axis, backward)
        block = jnp.concatenate([low, block, high], axis=dim)
    return block


def spectral_table(lon_width, col_count):
    wave_count = lon_width // 2 + 1
    col_ids = lax.broadcasted_iota(jnp.int32, (col_count, wave_count), 0)
    wave_ids = lax.broadcasted_iota(jnp.int32, (col_count, wave_count), 1)
    phase = (col_ids * wave_ids % lon_width).astype(jnp.float32) * (2.0 * math.pi / lon_width)
    return jnp.concatenate([jnp.cos(phase), jnp.sin(phase)], axis=1)


def row_factor(lat_rows, polar_mask, lon_width):
    total_rows = polar_mask.shape[0]
    polar_most = total_rows // 8
    south_count = jnp.sum(polar_mask[: total_rows // 2])
    north_count = jnp.sum(polar_mask[total_rows // 2 :])
    live_rows = (lat_rows < south_count) | (lat_rows >= total_rows - north_count)
    cosine = jnp.sin(math.pi * (lat_rows.astype(jnp.float32) + 0.5) / total_rows)
    lat_ratio = cosine / math.sin(math.pi * polar_most / total_rows)
    wavenum = jnp.arange(lon_width // 2 + 1, dtype=jnp.float32)
    sine_k = jnp.sin(math.pi * wavenum / lon_width)
    damping = lat_ratio[:, None] / jnp.maximum(sine_k[None, :], lat_ratio[:, None])
    weights = jnp.where(
        (wavenum == 0) | (wavenum == lon_width // 2), 1.0 / lon_width, 2.0 / lon_width
    )
    factor = jnp.where(live_rows[:, None], (damping - 1.0) * weights[None, :], 0.0)
    return jnp.concatenate([factor, factor], axis=1)


def filter_rows(row_data, factor, basis):
    spectra = jnp.dot(row_data, basis, precision=precise_mode)
    correction = lax.dot_general(
        spectra * factor, basis, (((1,), (1,)), ((), ())), precision=precise_mode
    )
    return row_data + correction


def shards(
    adjoint_in, wind_east, wind_north, polar_mask, obs_owner, obs_cell, obs_kernel, obs_resid
):
    tracers, levels, lat_dev, lon_dev = adjoint_in.shape
    lat_count = lax.axis_size("lat")
    lon_count = lax.axis_size("lon")
    lat_index = lax.axis_index("lat")
    lon_index = lax.axis_index("lon")
    lon_width = lon_dev * lon_count
    total_rows = lat_dev * lat_count
    local_rows = lat_index * lat_dev + lax.broadcasted_iota(jnp.int32, (1, lat_dev, 1), 1)
    north_wind = jnp.where(local_rows < total_rows - 1, wind_north, 0.0)
    wind_stack = jnp.concatenate([wind_east, north_wind], axis=0)
    devices = lat_count * lon_count
    obs_count = obs_owner.shape[0]
    capacity = 2 * obs_count // devices
    owner_dev = obs_owner[:, 0]
    one_hot = (owner_dev[:, None] == lax.broadcasted_iota(jnp.int32, (1, devices), 1)).astype(
        jnp.int32
    )
    position = jnp.sum(jnp.cumsum(one_hot, axis=0) * one_hot, axis=1) - 1
    slot_index = owner_dev * capacity + position
    sounding_values = (obs_resid[:, :, None] * obs_kernel[:, None, :]).reshape(
        obs_count, tracers * levels
    )
    send_values = (
        jnp.zeros((devices * capacity, tracers * levels), jnp.float32)
        .at[slot_index]
        .set(sounding_values)
    )
    send_cells = jnp.zeros((devices * capacity,), jnp.int32).at[slot_index].set(obs_cell)
    send_values = send_values.reshape(lat_count, lon_count, capacity, tracers * levels)
    send_cells = send_cells.reshape(lat_count, lon_count, capacity)
    got_values, got_cells = (
        lax.all_to_all(
            lax.all_to_all(send_values, "lat", split_axis=0, concat_axis=0, tiled=True),
            "lon",
            split_axis=1,
            concat_axis=1,
            tiled=True,
        ),
        lax.all_to_all(
            lax.all_to_all(send_cells, "lat", split_axis=0, concat_axis=0, tiled=True),
            "lon",
            split_axis=1,
            concat_axis=1,
            tiled=True,
        ),
    )
    got_values = got_values.reshape(devices * capacity, tracers * levels)
    got_cells = got_cells.reshape(devices * capacity)
    adjoint = adjoint_in.reshape(tracers * levels, lat_dev * lon_dev)
    adjoint = adjoint.at[:, got_cells].add(got_values.T)
    adjoint = adjoint.reshape(tracers * levels * lat_dev, lon_dev)
    rows_per = tracers * levels * lat_dev // lon_count
    grouped = lax.all_to_all(adjoint, "lon", split_axis=0, concat_axis=1, tiled=True)
    basis = spectral_table(lon_width, lon_width)
    flat_rows = lon_index * rows_per + jnp.arange(rows_per, dtype=jnp.int32)
    factor = row_factor(lat_index * lat_dev + flat_rows % lat_dev, polar_mask, lon_width)
    filtered = filter_rows(grouped, factor, basis)
    adjoint = lax.all_to_all(filtered, "lon", split_axis=1, concat_axis=0, tiled=True)
    adjoint = adjoint.reshape(tracers * levels, lat_dev, lon_dev)
    joint_padded = with_halo(
        jnp.concatenate([adjoint, wind_stack], axis=0), (("lat", 1), ("lon", 2)), 1
    )
    field_padded = joint_padded[: tracers * levels]
    wind_padded = joint_padded[tracers * levels :]
    shape_four = (tracers, levels, lat_dev, lon_dev)
    center = field_padded[:, 1:-1, 1:-1].reshape(shape_four)
    east_val = field_padded[:, 1:-1, 2:].reshape(shape_four)
    west_val = field_padded[:, 1:-1, :-2].reshape(shape_four)
    upper_val = field_padded[:, 2:, 1:-1].reshape(shape_four)
    lower_val = field_padded[:, :-2, 1:-1].reshape(shape_four)
    east_face = jnp.maximum(wind_padded[:levels, 1:-1, 1:-1], 0.0)
    west_face = jnp.minimum(wind_padded[:levels, 1:-1, :-2], 0.0)
    north_face = jnp.maximum(wind_padded[levels:, 1:-1, 1:-1], 0.0)
    south_face = jnp.minimum(wind_padded[levels:, :-2, 1:-1], 0.0)
    result = center + east_face * (east_val - center) + west_face * (center - west_val)
    return result + north_face * (upper_val - center) + south_face * (center - lower_val)


def solution(mesh):
    placed = (
        P(None, None, "lat", "lon"),
        P(None, "lat", "lon"),
        P(None, "lat", "lon"),
        P(),
        P(("lat", "lon"), None),
        P(("lat", "lon")),
        P(("lat", "lon"), None),
        P(("lat", "lon"), None),
    )
    return jax.shard_map(
        shards, mesh=mesh, in_specs=placed, out_specs=P(None, None, "lat", "lon"), check_vma=False
    )
```

profile of v0, /device:TPU:0, one launch (start us, length us, event | category | flops | bytes accessed | tf_op | source)
XLA Modules:
  0.0 476.2 jit_solution(6121776633378828527)
XLA Ops:
  0.8 9.2 %reduce-window.6 = s32[32,32,128]{2,1,0:T(8,128)S(1)} reduce-window(s32[32,32,128]{2,1,0:T(8,128)S(1)} %fusion.23, s32[]{:T(128)} %constant.27.clone.1), window={size=1x1x128 pad=0_0x0_0x127_0}, to_apply=%region_0.1 | reduce-window | flops 16646144 | bytes 1048580 | tf_op jit(solution)/shard_map/reduce-window
  11.7 15.7 %scatter_custom_fusion = s32[8192]{0:T(1024)S(1)} fusion(s32[4096]{0:T(1024)S(1)} %bitcast.52, s32[4096]{0:T(1024)} %param.13, s32[]{:T(128)} %constant.27.clone.1), kind=kCustom, calls=%fused_computation.72 | custom fusion | bytes 33280 | tf_op jit(solution)/shard_map/scatter | solution.py:89
  28.0 5.2 %all-to-all-start = ((s32[8,4,256]{2,1,0:T(4,128)}), s32[8,4,256]{2,1,0:T(4,128)S(1)}, u32[]{:S(2)}, u32[]{:S(2)}) async-start(s32[8,4,256]{2,1,0:T(4,128)} %reshape.154), calls=%async_computation | async-start | bytes 65536 | tf_op jit(solution)/shard_map/all_to_all | solution.py:101
  33.9 12.8 %scatter_custom_fusion.1 = f32[8192,48]{1,0:T(8,128)} fusion(s32[4096]{0:T(1024)S(1)} %bitcast.53, f32[4096,48]{1,0:T(8,128)S(1)} %copy.50, f32[]{:T(128)} %constant.33.clone.1), kind=kCustom, calls=%fused_computation.45 | custom fusion | bytes 1572868 | tf_op jit(solution)/shard_map/scatter | solution.py:87
  46.7 3.7 copy.51
  50.3 4.2 all-to-all-start.2
  55.1 20.4 %all-to-all-done.2 = f32[8,4,256,48]{2,3,1,0:T(8,128)S(1)} async-done(((f32[8,4,256,48]{2,3,1,0:T(8,128)}), f32[8,4,256,48]{2,3,1,0:T(8,128)S(1)}, u32[]{:S(2)}, u32[]{:S(2)}) %all-to-all-start.2) | async-done | bytes 1572896 | tf_op jit(solution)/shard_map/all_to_all | solution.py:94
  75.6 4.9 %all-to-all-start.1 = ((s32[8,4,256]{2,0,1:T(8,128)}), s32[8,4,256]{2,0,1:T(8,128)S(1)}, u32[]{:S(2)}, u32[]{:S(2)}) async-start(s32[8,4,256]{2,0,1:T(8,128)} %copy.48), calls=%async_computation.1 | async-start | bytes 65536 | tf_op jit(solution)/shard_map/all_to_all | solution.py:100
  81.7 4.4 all-to-all-done.1
  86.1 4.4 all-to-all-start.3
  93.0 3.9 copy.54
  97.0 26.6 %all-to-all-done.3 = f32[8,4,256,48]{2,3,0,1:T(8,128)} async-done(((f32[8,4,256,48]{2,3,0,1:T(8,128)}), f32[8,4,256,48]{2,3,0,1:T(8,128)}, u32[]{:S(2)}, u32[]{:S(2)}) %all-to-all-start.3) | async-done | bytes 1572896 | tf_op jit(solution)/shard_map/all_to_all | solution.py:93
  123.6 3.8 copy.75
  127.3 54.6 %scatter_fusion = f32[48,11520]{0,1:T(8,128)} fusion(f32[48,11520]{0,1:T(8,128)} %copy.54, s32[8192]{0:T(1024)S(1)} %bitcast.49, f32[8192,48]{1,0:T(8,128)} %bitcast.38), kind=kCustom, calls=%fused_computation.2 | custom fusion | flops 393216 | bytes 4751360 | tf_op jit(solution)/shard_map/scatter-add | solution.py:111
  181.9 4.2 copy.56
  186.1 3.2 all_to_all.42
  189.2 4.0 all-to-all-start.4
  195.7 74.8 %fusion.6 = (f32[2880,1441]{1,0:T(8,128)}, f32[2880,1441]{1,0:T(8,128)}) fusion(), kind=kLoop, calls=%fused_computation.12 | loop fusion | flops 37350720 | bytes 33200640 | tf_op jit(solution)/shard_map/sin | solution.py:30
  270.5 2.9 copy.57
  273.4 3.0 all_to_all.45
  276.4 38.0 %fusion.9 = f32[192,2882]{1,0:T(8,128)} fusion(f32[192,2880]{1,0:T(8,128)S(1)} %all_to_all.45, f32[2880,1441]{1,0:T(8,128)} %get-tuple-element.22, f32[2880,1441]{1,0:T(8,128)} %get-tuple-element.23, f32[192,1441]{1,0:T(8,128)S(1)} %multiply_select_fusion), kind=kOutput, calls=%fused_computation.15 | convolution fusion | flops 19132975104 | bytes 38732544 | tf_op jit(solution)/shard_map/dot_general | solution.py:52
  314.4 46.3 %fusion.10 = f32[192,2880]{1,0:T(8,128)} fusion(f32[192,2880]{1,0:T(8,128)S(1)} %all_to_all.45, f32[192,2882]{1,0:T(8,128)} %fusion.9, f32[2880,1441]{1,0:T(8,128)} %get-tuple-element.22, f32[2880,1441]{1,0:T(8,128)} %get-tuple-element.23), kind=kOutput, calls=%fused_computation.16 | convolution fusion | flops 19132422144 | bytes 39837696 | tf_op jit(solution)/shard_map/dot_general | solution.py:53
  360.7 3.4 all_to_all.46
  366.0 5.1 %all-to-all-start.5 = ((f32[192,4,720]{2,0,1:T(8,128)}), f32[192,4,720]{2,0,1:T(8,128)S(1)}, u32[]{:S(2)}, u32[]{:S(2)}) async-start(f32[192,4,720]{2,0,1:T(8,128)} %copy.58), calls=%async_computation.5 | async-start | bytes 4718592 | tf_op jit(solution)/shard_map/all_to_all | solution.py:119
  371.1 4.5 broadcast_maximum_fusion
  375.6 50.3 %all-to-all-done.5 = f32[192,4,720]{2,0,1:T(8,128)S(1)} async-done(((f32[192,4,720]{2,0,1:T(8,128)}), f32[192,4,720]{2,0,1:T(8,128)S(1)}, u32[]{:S(2)}, u32[]{:S(2)}) %all-to-all-start.5) | async-done | bytes 2211872 | tf_op jit(solution)/shard_map/all_to_all | solution.py:119
  427.3 3.1 copy.62
  430.5 2.9 collective-permute-start.1
  438.9 3.4 collective-permute-done
  447.7 3.8 collective-permute-start.2
  462.7 5.8 %pad_maximum_fusion.18 = (f32[48,16,720]{2,0,1:T(8,128)S(1)}, f32[48,16,720]{2,0,1:T(8,128)S(1)}, f32[48,16,720]{2,0,1:T(8,128)S(1)}) fusion(f32[96,18,1]{2,0,1:T(8,128)} %copy.65, f32[96,1,720]{2,0,1:T(8,128)} %copy-done.4, f32[96,1,720]{2,0,1:T(8,128)} %copy-done.11, f32[24,16,720]{2,0,1:T(8,128)S(1)} %get-tuple-element.8, ...), kind=kLoop, calls=%fused_computation.28 | loop fusion | flops 7188480 | bytes 11625984 | tf_op jit(solution)/shard_map/concatenate | solution.py:21
  468.6 7.1 %fusion.12 = f32[2,24,16,720]{3,2,1,0:T(8,128)} fusion(f32[2,24,16,720]{3,2,1,0:T(8,128)S(1)} %bitcast.37, f32[2,24,16,720]{3,1,0,2:T(8,128)S(1)} %bitcast.43, f32[2,24,16,720]{3,1,0,2:T(8,128)S(1)} %bitcast.40, f32[2,24,16,720]{3,1,0,2:T(8,128)S(1)} %bitcast.42, f32[2,24,16,720]{3,1,0,2:T(8,128)S(1)} %bitcast.41, f32[24,16,720]{2,1,0:T(8,128)S(1)} %copy-done.8, ...), kind=kLoop, calls=%fused_computation.35 | loop fusion | flops 6635520 | bytes 17694720 | tf_op jit(solution)/shard_map/add | solution.py:137
  (74 shorter events, 35.3 us)
Async XLA Ops:
  0.0 11.3 %copy-start.13 = (s32[4096,1]{0,1:T(1,128)S(1)}, s32[4096,1]{0,1:T(1,128)}, u32[]{:S(2)}) copy-start(s32[4096,1]{0,1:T(1,128)} %param.12) | copy-start | bytes 49156
  0.0 33.2 %copy-start.12 = (f32[4096,24]{0,1:T(8,128)S(1)}, f32[4096,24]{0,1:T(8,128)}, u32[]{:S(2)}) copy-start(f32[4096,24]{0,1:T(8,128)} %param.14) | copy-start | bytes 1179652
  0.0 33.2 %copy-start.14 = (f32[4096,2]{0,1:T(2,128)S(1)}, f32[4096,2]{0,1:T(2,128)}, u32[]{:S(2)}) copy-start(f32[4096,2]{0,1:T(2,128)} %param.15) | copy-start | bytes 98308
  28.0 22.3 %all-to-all-start = ((s32[8,4,256]{2,1,0:T(4,128)}), s32[8,4,256]{2,1,0:T(4,128)S(1)}, u32[]{:S(2)}, u32[]{:S(2)}) async-start(s32[8,4,256]{2,1,0:T(4,128)} %reshape.154), calls=%async_computation | async-start | bytes 65536 | tf_op jit(solution)/shard_map/all_to_all | solution.py:101
  50.3 25.2 %all-to-all-start.2 = ((f32[8,4,256,48]{2,3,1,0:T(8,128)}), f32[8,4,256,48]{2,3,1,0:T(8,128)S(1)}, u32[]{:S(2)}, u32[]{:S(2)}) async-start(f32[8,4,256,48]{2,3,1,0:T(8,128)} %copy.51), calls=%async_computation.2 | async-start | bytes 3145728 | tf_op jit(solution)/shard_map/all_to_all | solution.py:94
  75.6 10.5 %all-to-all-start.1 = ((s32[8,4,256]{2,0,1:T(8,128)}), s32[8,4,256]{2,0,1:T(8,128)S(1)}, u32[]{:S(2)}, u32[]{:S(2)}) async-start(s32[8,4,256]{2,0,1:T(8,128)} %copy.48), calls=%async_computation.1 | async-start | bytes 65536 | tf_op jit(solution)/shard_map/all_to_all | solution.py:100
  86.1 37.5 %all-to-all-start.3 = ((f32[8,4,256,48]{2,3,0,1:T(8,128)}), f32[8,4,256,48]{2,3,0,1:T(8,128)}, u32[]{:S(2)}, u32[]{:S(2)}) async-start(f32[8,4,256,48]{2,3,0,1:T(8,128)} %copy.52), calls=%async_computation.3 | async-start | bytes 3145728 | tf_op jit(solution)/shard_map/all_to_all | solution.py:93
  189.2 4.0 copy-start.15
  189.2 81.2 %all-to-all-start.4 = ((f32[4,192,720]{2,1,0:T(8,128)}), f32[4,192,720]{2,1,0:T(8,128)S(1)}, u32[]{:S(2)}, u32[]{:S(2)}) async-start(f32[4,192,720]{2,1,0:T(8,128)} %all_to_all.42), calls=%async_computation.4 | async-start | bytes 4718592 | tf_op jit(solution)/shard_map/all_to_all | solution.py:114
  366.0 59.9 %all-to-all-start.5 = ((f32[192,4,720]{2,0,1:T(8,128)}), f32[192,4,720]{2,0,1:T(8,128)S(1)}, u32[]{:S(2)}, u32[]{:S(2)}) async-start(f32[192,4,720]{2,0,1:T(8,128)} %copy.58), calls=%async_computation.5 | async-start | bytes 4718592 | tf_op jit(solution)/shard_map/all_to_all | solution.py:119
  425.9 1.4 copy-start.1
  427.3 3.1 copy-start
  430.5 3.0 copy-start.10
  430.5 4.4 copy-start.9
  430.5 8.3 %collective-permute-start.1 = (f32[96,1,720]{2,0,1:T(8,128)S(1)}, f32[96,1,720]{2,0,1:T(8,128)S(1)}, u32[]{:S(2)}, u32[]{:S(2)}) collective-permute-start(f32[96,1,720]{2,0,1:T(8,128)S(1)} %get-tuple-element.16), channel_id=1, source_target_pairs={{4,0},{8,4},{12,8},{16,12},{20,16},{24,20},{28,24},{0,28},{5,1},{9... | collective-permute-start | bytes 829448 | tf_op jit(solution)/shard_map/ppermute | solution.py:20
  433.5 8.8 %collective-permute-start = (f32[96,1,720]{2,0,1:T(8,128)S(1)}, f32[96,1,720]{2,0,1:T(8,128)S(1)}, u32[]{:S(2)}, u32[]{:S(2)}) collective-permute-start(f32[96,1,720]{2,0,1:T(8,128)S(1)} %get-tuple-element.17), channel_id=1, source_target_pairs={{0,4},{4,8},{8,12},{12,16},{16,20},{20,24},{24,28},{28,0},{1,5},{5... | collective-permute-start | bytes 829448 | tf_op jit(solution)/shard_map/ppermute | solution.py:17
  438.9 4.9 %copy-start.4 = (f32[96,1,720]{2,0,1:T(8,128)}, f32[96,1,720]{2,0,1:T(8,128)S(1)}, u32[]{:S(2)}) copy-start(f32[96,1,720]{2,0,1:T(8,128)S(1)} %collective-permute-done.1) | copy-start | bytes 829444
  442.3 1.5 copy-start.11
  445.9 8.1 %collective-permute-start.3 = (f32[96,18,1]{0,1,2:T(8,128)}, f32[96,18,1]{0,1,2:T(8,128)}, u32[]{:S(2)}, u32[]{:S(2)}) collective-permute-start(f32[96,18,1]{0,1,2:T(8,128)} %copy.67), channel_id=1, source_target_pairs={{0,1},{1,2},{2,3},{3,0},{4,5},{5,6},{6,7},{7,4},{8,9},{9,10},{10,1... | collective-permute-start | bytes 20744 | tf_op jit(solution)/shard_map/ppermute | solution.py:17
  447.7 13.0 %collective-permute-start.2 = (f32[96,18,1]{0,1,2:T(8,128)S(1)}, f32[96,18,1]{0,1,2:T(8,128)}, u32[]{:S(2)}, u32[]{:S(2)}) collective-permute-start(f32[96,18,1]{0,1,2:T(8,128)S(1)} %copy.64), channel_id=1, source_target_pairs={{1,0},{2,1},{3,2},{0,3},{5,4},{6,5},{7,6},{4,7},{9,8},{10,9},{11,1... | collective-permute-start | bytes 20744 | tf_op jit(solution)/shard_map/ppermute | solution.py:20
  462.7 5.9 %copy-start.2 = (f32[192,4,720]{2,0,1:T(8,128)S(1)}, f32[192,4,720]{2,0,1:T(8,128)}, u32[]{:S(2)}) copy-start(f32[192,4,720]{2,0,1:T(8,128)} %copy-done.1) | copy-start | bytes 6635524
  462.7 5.9 %copy-start.3 = (f32[48,16,720]{2,0,1:T(8,128)S(1)}, f32[48,16,720]{2,0,1:T(8,128)}, u32[]{:S(2)}) copy-start(f32[48,16,720]{2,0,1:T(8,128)} %pad_maximum_fusion.10) | copy-start | bytes 6635524
  462.7 5.9 %copy-start.5 = (f32[24,16,720]{2,1,0:T(8,128)S(1)}, f32[24,16,720]{2,1,0:T(8,128)}, u32[]{:S(2)}) copy-start(f32[24,16,720]{2,1,0:T(8,128)} %copy.60) | copy-start | bytes 3317764
  462.7 5.9 %copy-start.6 = (f32[24,16,720]{2,1,0:T(8,128)S(1)}, f32[24,16,720]{2,1,0:T(8,128)}, u32[]{:S(2)}) copy-start(f32[24,16,720]{2,1,0:T(8,128)} %copy.71) | copy-start | bytes 3317764
  462.7 5.9 %copy-start.7 = (f32[24,16,720]{2,1,0:T(8,128)S(1)}, f32[24,16,720]{2,1,0:T(8,128)}, u32[]{:S(2)}) copy-start(f32[24,16,720]{2,1,0:T(8,128)} %copy.69) | copy-start | bytes 3317764
  462.7 5.9 %copy-start.8 = (f32[24,16,720]{2,1,0:T(8,128)S(1)}, f32[24,16,720]{2,1,0:T(8,128)}, u32[]{:S(2)}) copy-start(f32[24,16,720]{2,1,0:T(8,128)} %copy.73) | copy-start | bytes 3317764
where the time goes:
time: 485 us; the launch traced here: 476 us
  other arithmetic  165 us (34%)
  waiting for transfers between devices  108 us (22%)
  matrix products  84.3 us (17%)
  local copies, waits for them, and re-layouts  82.7 us (17%)
  starting transfers between devices  34.7 us (7%)
    sin x1, other arithmetic, spectral_table(): return jnp.concatenate([jnp.cos(phase), jnp.sin(phase)], axis=1)  74.8 us
    scatter-add x1, other arithmetic, shards(): adjoint = adjoint.at[:, got_cells].add(got_values.T)  54.6 us
    all_to_all x1, waiting for transfers between devices, shards(): lax.all_to_all(filtered, 'lon', split_axis=1, concat_axis=0, tiled=True)  50.3 us
    dot_general x1, matrix products, filter_rows(): lax.dot_general(spectra * factor, basis, (((1,), (1,)), ((), ())), precis...  46.3 us
    dot_general x1, matrix products, filter_rows(): spectra = jnp.dot(row_data, basis, precision=precise_mode)  38 us
    all_to_all x1, waiting for transfers between devices, shards(): lax.all_to_all(lax.all_to_all(send_values, 'lat', split_axis=0, concat_ax...  26.6 us
    all_to_all x1, waiting for transfers between devices, shards(): lax.all_to_all(send_values, 'lat', split_axis=0, concat_axis=0, tiled=True)  20.4 us
    scatter x1, local copies, waits for them, and re-layouts, shards(): jnp.zeros((devices * capacity,), jnp.int32).at[slot_index].set(obs_cell)  15.7 us
  transfers between devices with their start and end apart: 10, of which 6 were waited for; matrix products, arithmetic and copies ran while one was open for 25% of the time, Pallas kernels for 0%

commit v1 on v0

v1 whole, which is shorter than its diff:
```python
import functools
import math

import jax
import jax.numpy as jnp
import numpy as np
from jax import lax
from jax.experimental import pallas as pl
from jax.experimental.pallas import tpu as pltpu
from jax.sharding import PartitionSpec as P

precise_mode = lax.Precision.HIGH
ACCS = 4
UNROLL = 4


def circle_tables(lon_width):
    width = lon_width // 4
    half = width // 2
    inner = 16

    def table(waves, turns, repeats):
        high = np.arange(width // inner)[:, None] * inner
        high = 2.0 * np.pi * ((high * waves[None, :]) % lon_width) / lon_width
        high = np.concatenate([high + 0.5 * np.pi * turn for turn in range(repeats)], 0)
        low = np.arange(inner)[:, None]
        low = 2.0 * np.pi * ((low * waves[None, :]) % lon_width) / lon_width
        low = low - 0.5 * np.pi * turns[None, :]
        parts = [np.cos(high), np.sin(high), np.cos(low), np.sin(low)]
        parts = lax.optimization_barrier([jnp.asarray(part.astype(np.float32)) for part in parts])
        cos_high, sin_high, cos_low, sin_low = parts
        full = cos_high[:, None] * cos_low[None] - sin_high[:, None] * sin_low[None]
        return full.reshape(repeats * width, waves.shape[0])

    zero = np.concatenate([4 * np.arange(half + 1), 4 * np.arange(1, half)])
    zero_turns = np.concatenate([np.zeros(half + 1), np.ones(half - 1)])
    zero_weights = np.where((zero == 0) | (zero == lon_width // 2), 1.0, 2.0)
    two = np.tile(4 * np.arange(half) + 2, 2)
    one = np.tile(4 * np.arange(width) + 1, 2)
    return [
        (table(zero, zero_turns, 1), zero, zero_weights / lon_width),
        (table(two, np.repeat([0, 1], half), 1), two, np.full(width, 2.0 / lon_width)),
        (table(one, np.repeat([0, 1], width), 2), one, np.full(2 * width, 2.0 / lon_width)),
    ]


def corrected(data, basis, waves, weights, lat_ratio, live, lon_width):
    fields, rows, width = data.shape
    sine_k = jnp.asarray(np.sin(np.pi * waves / lon_width).astype(np.float32))
    damping = lat_ratio[:, None] / jnp.maximum(sine_k[None, :], lat_ratio[:, None])
    factor = (damping - 1.0) * jnp.asarray(weights.astype(np.float32))[None, :]
    factor = jnp.where(live[:, None], factor, 0.0)
    spectra = jnp.dot(data.reshape(fields * rows, width), basis, precision=precise_mode)
    spectra = (spectra.reshape(fields, rows, width) * factor[None]).reshape(fields * rows, width)
    result = lax.dot_general(spectra, basis, (((1,), (1,)), ((), ())), precision=precise_mode)
    return result.reshape(fields, rows, width)


def scatter_kernel(cells_ref, values_ref, out_ref, *extra):
    accs = (out_ref,) + extra
    total, width = out_ref.shape
    chunk = 64
    count = values_ref.shape[0]

    def clear(i, carry):
        where = pl.ds(pl.multiple_of(i * chunk, chunk), chunk)
        for acc in accs:
            acc[where, :] = jnp.zeros((chunk, width), jnp.float32)
        return carry

    lax.fori_loop(0, total // chunk, clear, 0)
    step = ACCS * UNROLL

    def add(i, carry):
        base = i * step
        for turn in range(UNROLL):
            places, olds = [], []
            for lane in range(ACCS):
                place = cells_ref[base + turn * ACCS + lane]
                places.append(place)
                olds.append(
                    accs[lane][pl.ds(place, 1), :]
                    + values_ref[pl.ds(base + turn * ACCS + lane, 1), :]
                )
            for lane in range(ACCS):
                accs[lane][pl.ds(places[lane], 1), :] = olds[lane]
        return carry

    lax.fori_loop(0, count // step, add, 0)

    def join(i, carry):
        where = pl.ds(pl.multiple_of(i * chunk, chunk), chunk)
        total_here = accs[0][where, :]
        for acc in extra:
            total_here = total_here + acc[where, :]
        out_ref[where, :] = total_here
        return carry

    lax.fori_loop(0, total // chunk, join, 0)


def add_soundings(cells, values, total):
    width = values.shape[1]
    return pl.pallas_call(
        scatter_kernel,
        out_shape=jax.ShapeDtypeStruct((total, width), jnp.float32),
        in_specs=[
            pl.BlockSpec(memory_space=pltpu.SMEM),
            pl.BlockSpec(memory_space=pltpu.VMEM),
        ],
        out_specs=pl.BlockSpec(memory_space=pltpu.VMEM),
        scratch_shapes=[pltpu.VMEM((total, width), jnp.float32)] * (ACCS - 1),
        compiler_params=pltpu.CompilerParams(vmem_limit_bytes=48 * 1024 * 1024),
    )(cells, values)


def stencil_kernel(
    field_ref, east_ref, north_ref, east_col, west_col, north_row, south_row,
    wind_col, wind_row, out_ref, wide,
):
    tracers, levels, rows, width = field_ref.shape
    padded = wide.shape[1]
    lanes = lax.broadcasted_iota(jnp.int32, (rows, padded), 1)
    subs = lax.broadcasted_iota(jnp.int32, (rows, padded), 0)

    def widened(slot, block):
        wide[slot * rows : (slot + 1) * rows, 0:width] = block
        return wide[slot * rows : (slot + 1) * rows, :]

    def wide_row(slot, block):
        wide[slot * rows : slot * rows + 1, 0:width] = block
        return wide[slot * rows : slot * rows + 1, :]

    for level in range(levels):
        wind_east = widened(0, east_ref[level])
        wind_west = jnp.where(lanes == 0, wind_col[level], pltpu.roll(wind_east, 1, 1))
        wind_north = widened(1, north_ref[level])
        wind_south = jnp.where(
            subs == 0, wide_row(2, wind_row[level]), pltpu.roll(wind_north, 1, 0)
        )
        east_face = jnp.maximum(wind_east, 0.0)
        west_face = jnp.minimum(wind_west, 0.0)
        north_face = jnp.maximum(wind_north, 0.0)
        south_face = jnp.minimum(wind_south, 0.0)
        for tracer in range(tracers):
            center = widened(3 + 3 * tracer, field_ref[tracer, level])
            east_val = jnp.where(
                lanes == width - 1, east_col[tracer, level], pltpu.roll(center, padded - 1, 1)
            )
            west_val = jnp.where(lanes == 0, west_col[tracer, level], pltpu.roll(center, 1, 1))
            upper_val = jnp.where(
                subs == rows - 1,
                wide_row(4 + 3 * tracer, north_row[tracer, level]),
                pltpu.roll(center, rows - 1, 0),
            )
            lower_val = jnp.where(
                subs == 0,
                wide_row(5 + 3 * tracer, south_row[tracer, level]),
                pltpu.roll(center, 1, 0),
            )
            result = center + east_face * (east_val - center) + west_face * (center - west_val)
            result = result + north_face * (upper_val - center) + south_face * (center - lower_val)
            out_ref[tracer, level] = result[:, 0:width]


def advect(field, wind_east, wind_north, east_col, west_col, north_row, south_row, wind_col, wind_row):
    tracers, levels, rows, width = field.shape
    step = 4 if levels % 4 == 0 else 1

    def four(depth, span):
        return pl.BlockSpec((tracers, step, depth, span), lambda i: (0, i, 0, 0))

    def three(depth, span):
        return pl.BlockSpec((step, depth, span), lambda i: (i, 0, 0))

    padded = -(-(width + 1) // 128) * 128
    return pl.pallas_call(
        stencil_kernel,
        grid=(levels // step,),
        out_shape=jax.ShapeDtypeStruct(field.shape, jnp.float32),
        in_specs=[
            four(rows, width), three(rows, width), three(rows, width),
            four(rows, 1), four(rows, 1), four(1, width), four(1, width),
            three(rows, 1), three(1, width),
        ],
        out_specs=four(rows, width),
        scratch_shapes=[pltpu.VMEM(((3 + 3 * tracers) * rows, padded), jnp.float32)],
        compiler_params=pltpu.CompilerParams(vmem_limit_bytes=32 * 1024 * 1024),
    )(field, wind_east, wind_north, east_col, west_col, north_row, south_row, wind_col, wind_row)


def owner_positions(owner_dev, devices):
    count = owner_dev.shape[0]
    span = 128
    one_hot = (owner_dev[:, None] == lax.broadcasted_iota(jnp.int32, (1, devices), 1)).astype(
        jnp.bfloat16
    ).reshape(count // span, span, devices)
    lower = jnp.asarray(np.tril(np.ones((span, span))), jnp.bfloat16)
    inner = jnp.einsum("ij,bjd->bid", lower, one_hot, preferred_element_type=jnp.float32)
    sums = inner[:, -1, :]
    blocks = count // span
    before = jnp.asarray(np.tril(np.ones((blocks, blocks)), -1), jnp.float32)
    offset = jnp.dot(before, sums, precision=lax.Precision.HIGHEST)
    ranks = (inner + offset[:, None, :]) * one_hot.astype(jnp.float32)
    return jnp.sum(ranks, axis=2).reshape(count).astype(jnp.int32) - 1


def shards(
    adjoint_in, wind_east, wind_north, polar_mask, obs_owner, obs_cell, obs_kernel, obs_resid
):
    tracers, levels, lat_dev, lon_dev = adjoint_in.shape
    fields = tracers * levels
    lat_count = lax.axis_size("lat")
    lon_count = lax.axis_size("lon")
    lat_index = lax.axis_index("lat")
    lon_width = lon_dev * lon_count
    total_rows = lat_dev * lat_count
    devices = lat_count * lon_count
    obs_count = obs_owner.shape[0]
    capacity = 2 * obs_count // devices

    owner_dev = obs_owner[:, 0]
    slot_index = owner_dev * capacity + owner_positions(owner_dev, devices)
    payload = jnp.concatenate(
        [
            obs_kernel,
            obs_resid,
            obs_cell.astype(jnp.float32)[:, None],
            jnp.zeros((obs_count, 32 - levels - tracers - 1), jnp.float32),
        ],
        axis=1,
    )
    send = jnp.zeros((devices * capacity, 32), jnp.float32).at[slot_index].set(
        payload, unique_indices=True
    )
    got = lax.all_to_all(
        send.reshape(devices, capacity, 32), ("lat", "lon"), split_axis=0, concat_axis=0, tiled=True
    ).reshape(devices * capacity, 32)
    got_cells = got[:, levels + tracers].astype(jnp.int32)
    got_values = (
        got[:, levels : levels + tracers, None] * got[:, None, :levels]
    ).reshape(devices * capacity, fields)
    forcing = add_soundings(got_cells, got_values, lat_dev * lon_dev)
    adjoint = (
        adjoint_in.reshape(fields, lat_dev, lon_dev)
        + forcing.T.reshape(fields, lat_dev, lon_dev)
    )

    local_rows = lat_index * lat_dev + jnp.arange(lat_dev, dtype=jnp.int32)
    north_wind = jnp.where(local_rows[None, :, None] < total_rows - 1, wind_north, 0.0)
    up = [(i, i + 1) for i in range(lat_count - 1)]
    down = [(i + 1, i) for i in range(lat_count - 1)]
    east = [(i, (i + 1) % lon_count) for i in range(lon_count)]
    west = [((i + 1) % lon_count, i) for i in range(lon_count)]
    wind_row = lax.ppermute(north_wind[:, -1, :], "lat", up)[:, None, :]
    wind_col = lax.ppermute(wind_east[:, :, -1], "lon", east)[:, :, None]

    grouped = lax.all_to_all(
        adjoint.reshape(lon_count, fields // lon_count, lat_dev, lon_dev),
        "lon", split_axis=0, concat_axis=0, tiled=True,
    )
    lat_ratio = jnp.sin(math.pi * (local_rows.astype(jnp.float32) + 0.5) / total_rows) / math.sin(
        math.pi * (total_rows // 8) / total_rows
    )
    live = lax.dynamic_slice_in_dim(polar_mask, lat_index * lat_dev, lat_dev) > 0
    tables = circle_tables(lon_width)
    blocks = lon_count // 4
    quarters = [
        jnp.concatenate([grouped[blocks * i + j] for j in range(blocks)], axis=2) for i in range(4)
    ]
    quarter = lon_dev * blocks
    sum_even, sum_odd = quarters[0] + quarters[2], quarters[1] + quarters[3]
    pair = jnp.concatenate([quarters[0] - quarters[2], quarters[1] - quarters[3]], axis=2)
    filt = functools.partial(corrected, lat_ratio=lat_ratio, live=live, lon_width=lon_width)
    zero_part = filt(sum_even + sum_odd, *tables[0])
    two_part = filt(sum_even - sum_odd, *tables[1])
    pair_part = filt(pair, *tables[2])
    first, second = pair_part[:, :, :quarter], pair_part[:, :, quarter:]
    even_part, odd_part = zero_part + two_part, zero_part - two_part
    results = [
        quarters[0] + (even_part + first),
        quarters[1] + (odd_part + second),
        quarters[2] + (even_part - first),
        quarters[3] + (odd_part - second),
    ]
    filtered = jnp.stack(
        [
            result[:, :, j * lon_dev : (j + 1) * lon_dev]
            for result in results
            for j in range(blocks)
        ]
    )
    field = lax.all_to_all(filtered, "lon", split_axis=0, concat_axis=0, tiled=True)
    field = field.reshape(tracers, levels, lat_dev, lon_dev)

    north_row = lax.ppermute(field[:, :, 0, :], "lat", down)[:, :, None, :]
    south_row = lax.ppermute(field[:, :, -1, :], "lat", up)[:, :, None, :]
    east_col = lax.ppermute(field[:, :, :, 0], "lon", west)[..., None]
    west_col = lax.ppermute(field[:, :, :, -1], "lon", east)[..., None]
    return advect(
        field, wind_east, north_wind, east_col, west_col, north_row, south_row, wind_col, wind_row
    )


def solution(mesh):
    placed = (
        P(None, None, "lat", "lon"),
        P(None, "lat", "lon"),
        P(None, "lat", "lon"),
        P(),
        P(("lat", "lon"), None),
        P(("lat", "lon")),
        P(("lat", "lon"), None),
        P(("lat", "lon"), None),
    )

    return jax.shard_map(
        shards, mesh=mesh, in_specs=placed, out_specs=P(None, None, "lat", "lon"), check_vma=False
    )
```

time: 485 us -> 268 us (0.55); the launches traced: 476 us -> 267 us
  other arithmetic: 165 us -> 18.7 us
  matrix products: 84.3 us -> 22.4 us
  blocking collectives: 0 us -> 32.2 us
  local copies, waits for them, and re-layouts: 82.7 us -> 53.1 us
  Pallas kernels: 0 us -> 23.9 us
  waiting for transfers between devices: 108 us -> 93.4 us
  starting transfers between devices: 34.7 us -> 22.4 us
    sin x2 -> x0, other arithmetic: 74.9 us -> none  [the longest x1 74.8 us: spectral_table(): return jnp.concatenate([jnp.cos(phase), jnp.sin(phase)], axis=1)]
    dot_general x2 -> x8, matrix products: 84.3 us -> 22.4 us  [the longest x3 11.8 us: corrected(): jnp.dot(data.reshape(fields * rows, width), basis, precision=precise_mode)]
    scatter-add x1 -> x0, other arithmetic: 54.6 us -> none  [shards(): adjoint = adjoint.at[:, got_cells].add(got_values.T)]
    all_to_all x0 -> x1, blocking collectives: none -> 32.2 us  [shards(): lax.all_to_all(send.reshape(devices, capacity, 32), ('lat', 'lon'), split...]
    pallas_call x0 -> x2, Pallas kernels: none -> 23.9 us  [the longest x1 19.7 us: add_soundings(): pl.pallas_call(scatter_kernel, out_shape=jax.ShapeDtypeStruct((total, wid...]
    all_to_all x6 -> x2, starting transfers between devices: 27.7 us -> 11 us  [the longest x1 7.01 us: shards(): lax.all_to_all(adjoint.reshape(lon_count, fields // lon_count, lat_dev, l...]
    all_to_all x8 -> x0, local copies, waits for them, and re-layouts: 16.2 us -> none  [the longest x3 9.08 us: shards(): lax.all_to_all(adjoint, 'lon', split_axis=0, concat_axis=1, tiled=True)]
    scatter x2 -> x1, local copies, waits for them, and re-layouts: 28.5 us -> 12.8 us  [shards(): jnp.zeros((devices * capacity, 32), jnp.float32).at[slot_index]]
  transfers between devices with their start and end apart: 10 -> 8, of which waited for: 6 -> 2; matrix products, arithmetic and copies ran while one was open for 25% -> 8% of each run, Pallas kernels for 0% -> 0%
where the time goes in v1:
time: 268 us; the launch traced here: 267 us
  waiting for transfers between devices  93.4 us (35%)
  local copies, waits for them, and re-layouts  53.1 us (20%)
  blocking collectives  32.2 us (12%)
  Pallas kernels  23.9 us (9%)
  matrix products  22.4 us (8%)
  starting transfers between devices  22.4 us (8%)
  other arithmetic  18.7 us (7%)
    all_to_all x1, waiting for transfers between devices, shards(): lax.all_to_all(adjoint.reshape(lon_count, fields // lon_count, lat_dev, l...  46.9 us
    all_to_all x1, waiting for transfers between devices, shards(): lax.all_to_all(filtered, 'lon', split_axis=0, concat_axis=0, tiled=True)  46.5 us
    all_to_all x1, blocking collectives, shards(): lax.all_to_all(send.reshape(devices, capacity, 32), ('lat', 'lon'), split...  32.2 us
    pallas_call x1, Pallas kernels, add_soundings(): pl.pallas_call(scatter_kernel, out_shape=jax.ShapeDtypeStruct((total, wid...  19.7 us
    scatter x1, local copies, waits for them, and re-layouts, shards(): jnp.zeros((devices * capacity, 32), jnp.float32).at[slot_index]  12.8 us
    dot_general x3, matrix products, corrected(): jnp.dot(data.reshape(fields * rows, width), basis, precision=precise_mode)  11.8 us
    unnamed x59, local copies, waits for them, and re-layouts  11.2 us
    dot_general x3, matrix products, corrected(): lax.dot_general(spectra, basis, (((1,), (1,)), ((), ())), precision=preci...  8.74 us
  transfers between devices with their start and end apart: 8, of which 2 were waited for; matrix products, arithmetic and copies ran while one was open for 8% of the time, Pallas kernels for 0%

profile of v1, /device:TPU:0, one launch (start us, length us, event | category | flops | bytes accessed | tf_op | source)
XLA Modules:
  0.0 266.5 jit_solution(2156616646013688670)
XLA Ops:
  6.5 12.8 %scatter_custom_fusion = f32[8192,32]{1,0:T(8,128)} fusion(s32[4096]{0:T(1024)S(1)} %bitcast.107, f32[4096,32]{1,0:T(8,128)S(1)} %copy.80, f32[]{:T(128)} %constant.33.clone.1), kind=kCustom, calls=%fused_computation.6 | custom fusion | bytes 1048580 | tf_op jit(solution)/shard_map/scatter | solution.py:233
  19.3 2.8 %copy.81 = f32[32,256,32]{1,2,0:T(8,128)S(1)} copy(f32[32,256,32]{2,1,0:T(8,128)} %bitcast.95) | data formatting | bytes 2097152 | tf_op jit(solution)/shard_map/reshape | solution.py:237
  22.1 32.2 %all_to_all.15 = f32[32,256,32]{1,2,0:T(8,128)S(1)} all-to-all(f32[32,256,32]{1,2,0:T(8,128)S(1)} %copy.81), channel_id=1, replica_groups=mesh['lat'=8,'lon'=4] {'lat','lon'}, dimensions={0} | all-to-all | bytes 2097152 | tf_op jit(solution)/shard_map/all_to_all | solution.py:236
  54.6 2.7 %copy.83.values_ref = f32[8192,48]{1,0:T(8,128)} copy(f32[8192,48]{0,1:T(8,128)S(1)} %bitcast.96) | data formatting | bytes 3145728 | tf_op jit(solution)/shard_map/mul | solution.py:241
  57.3 2.2 copy-done
  59.5 19.7 %shard_map.262 = f32[11520,48]{1,0:T(8,128)} custom-call(s32[8192]{0:T(1024)S(1)} %bitcast.87, f32[8192,48]{1,0:T(8,128)S(1)} %copy-done), custom_call_target="tpu_custom_call" | custom-call | tf_op jit(solution)/shard_map/pallas_call | solution.py:104
  79.2 5.6 %copy.84 = f32[48,11520]{1,0:T(8,128)} copy(f32[48,11520]{0,1:T(8,128)} %bitcast.90) | data formatting | bytes 4423680 | tf_op jit(solution)/shard_map/transpose | solution.py:246
  84.8 3.3 %reshape.410 = f32[4,12,16,720]{3,2,1,0:T(8,128)S(1)} reshape(f32[48,11520]{1,0:T(8,128)} %copy.84) | data formatting | bytes 4423680 | tf_op jit(solution)/shard_map/reshape | solution.py:246
  88.1 3.4 %add.123 = f32[4,12,16,720]{3,2,1,0:T(8,128)} add(f32[4,12,16,720]{3,2,1,0:T(8,128)} %bitcast.101, f32[4,12,16,720]{3,2,1,0:T(8,128)S(1)} %reshape.410) | non-fusion elementwise | flops 552960 | bytes 6635520 | tf_op jit(solution)/shard_map/add | solution.py:245
  91.7 7.0 %all-to-all-start.1 = ((f32[4,12,16,720]{3,2,1,0:T(8,128)}), f32[4,12,16,720]{3,2,1,0:T(8,128)}, u32[]{:S(2)}, u32[]{:S(2)}) async-start(f32[4,12,16,720]{3,2,1,0:T(8,128)} %add.123), calls=%async_computation.1 | async-start | bytes 4718592 | tf_op jit(solution)/shard_map/all_to_all | solution.py:258
  99.7 1.8 multiply_subtract_fusion.1
  101.6 4.9 %multiply_subtract_fusion = f32[90,16,1440]{2,1,0:T(8,128)} fusion(f32[16,1440]{1,0:T(8,128)S(1)} %copy-done.17, f32[90,1440]{1,0:T(8,128)S(1)} %copy-done.11, f32[16,1440]{1,0:T(8,128)S(1)} %copy-done.16, f32[90,1440]{1,0:T(8,128)S(1)} %copy-done.10), kind=kLoop, calls=%fused_computation.1 | loop fusion | flops 6220800 | bytes 9515520 | tf_op jit(solution)/shard_map/sub | solution.py:32
  106.6 46.9 %all-to-all-done.1 = f32[4,12,16,720]{3,2,1,0:T(8,128)} async-done(((f32[4,12,16,720]{3,2,1,0:T(8,128)}), f32[4,12,16,720]{3,2,1,0:T(8,128)}, u32[]{:S(2)}, u32[]{:S(2)}) %all-to-all-start.1) | async-done | bytes 2211872 | tf_op jit(solution)/shard_map/all_to_all | solution.py:258
  153.4 1.7 bitcast_subtract_fusion.1
  155.2 6.4 %convolution_multiply_fusion = f32[12,16,1440]{2,1,0:T(8,128)S(1)} fusion(f32[1440,1440,1]{1,0,2:T(8,128)} %bitcast.88, f32[12,16,720]{2,1,0:T(8,128)S(1)} %get-tuple-element.38, f32[12,16,720]{2,1,0:T(8,128)S(1)} %get-tuple-element.37, f32[16,1440]{1,0:T(8,128)S(1)} %multiply_select_fusion), kind=kOutput, calls=%fused_computation.2 | convolution fusion | flops 2389340160 | bytes 10598400 | tf_op jit(solution)/shard_map/dot_general | solution.py:53
  161.6 4.6 %fusion.21 = f32[12,16,1440]{2,1,0:T(8,128)S(1)} fusion(f32[12,16,1440]{2,1,0:T(8,128)S(1)} %convolution_multiply_fusion, f32[1440,1440,1]{1,0,2:T(8,128)S(1)} %bitcast.89), kind=kOutput, calls=%fused_computation.56 | convolution fusion | flops 2388787200 | bytes 10506240 | tf_op jit(solution)/shard_map/dot_general | solution.py:55
  166.2 2.6 convolution_multiply_fusion.2
  170.5 2.8 %convolution_multiply_fusion.1 = f32[12,16,720]{2,1,0:T(8,128)S(1)} fusion(f32[720,720,1]{1,0,2:T(8,128)S(1)} %bitcast.93, f32[16,720]{1,0:T(8,128)S(1)} %get-tuple-element.39, f32[4,12,16,720]{3,2,1,0:T(8,128)} %all-to-all-done.1), kind=kOutput, calls=%fused_computation.8 | convolution fusion | flops 597749760 | bytes 4884480 | tf_op jit(solution)/shard_map/dot_general | solution.py:53
  173.3 3.0 %fusion.10 = (f32[1,12,16,720]{3,2,1,0:T(8,128)S(1)}, f32[1,12,16,720]{3,2,1,0:T(8,128)S(1)}, f32[1,12,16,720]{3,2,1,0:T(8,128)S(1)}, f32[1,12,16,720]{3,2,1,0:T(8,128)S(1)}) fusion(f32[12,16,1440]{2,1,0:T(8,128)S(1)} %fusion.21, f32[4,12,16,720]{3,2,1,0:T(8,128)} %all-to-all-done.1, f32[12,16,720]{2,1,0:T(8,128)S(1)} %fusion.20, ...), kind=kOutput, calls=%fused_computation.27 | convolution fusion | flops 598579200 | bytes 8709120 | tf_op jit(solution)/shard_map/dot_general | solution.py:55
  176.3 1.6 pad_maximum_fusion
  177.9 4.0 %all-to-all-start.2 = ((f32[4,12,16,720]{3,2,1,0:T(8,128)}), f32[4,12,16,720]{3,2,1,0:T(8,128)S(1)}, u32[]{:S(2)}, u32[]{:S(2)}) async-start(f32[4,12,16,720]{3,2,1,0:T(8,128)} %pad_maximum_fusion), calls=%async_computation.2 | async-start | bytes 4718592 | tf_op jit(solution)/shard_map/all_to_all | solution.py:293
  184.3 2.7 collective-permute-start.5
  188.2 1.7 collective-permute-start.4
  189.9 46.5 %all-to-all-done.2 = f32[4,12,16,720]{3,2,1,0:T(8,128)S(1)} async-done(((f32[4,12,16,720]{3,2,1,0:T(8,128)}), f32[4,12,16,720]{3,2,1,0:T(8,128)S(1)}, u32[]{:S(2)}, u32[]{:S(2)}) %all-to-all-start.2) | async-done | bytes 2211872 | tf_op jit(solution)/shard_map/all_to_all | solution.py:293
  239.3 3.7 %collective-permute-start.3 = (f32[2,24,720]{2,1,0:T(8,128)}, f32[2,24,720]{2,1,0:T(8,128)}, u32[]{:S(2)}, u32[]{:S(2)}) collective-permute-start(f32[2,24,720]{2,1,0:T(8,128)} %bitcast.82), channel_id=1, source_target_pairs={{0,4},{4,8},{8,12},{12,16},{16,20},{20,24},{24,28},{1,5},{5,9},{9,... | collective-permute-start | bytes 414728 | tf_op jit(solution)/shard_map/ppermute | solution.py:297
  243.4 1.4 collective-permute-start
  246.9 1.7 copy.91.north_ref
  248.5 1.5 copy.94.wind_col
  250.1 1.6 broadcast_in_dim.116.wind_row
  251.7 1.7 copy.92.east_col
  253.4 1.7 copy.93.west_col
  262.2 4.3 %shard_map.263 = f32[2,24,16,720]{3,2,1,0:T(8,128)} custom-call(f32[2,24,16,720]{3,2,1,0:T(8,128)S(1)} %bitcast.86, f32[24,16,720]{2,1,0:T(8,128)S(1)} %copy-done.1, f32[24,16,720]{2,1,0:T(8,128)S(1)} %copy.91.north_ref, f32[2,24,16,1]{3,2,1,0:T(8,128)S(1)} %copy-done.2, f32[2,24,16,1]{3,2,1,0:T(8,128)S(1)} %copy-done.3, ...), custom_call_target="tpu_custom_call" | custom-call | tf_op jit(solution)/shard_map/pallas_call | solution.py:177
  (98 shorter events, 25.5 us)
Async XLA Ops:
  57.3 2.2 copy-start
  91.6 7.2 %copy-start.27 = (s32[128]{0:T(128)S(1)}, s32[128]{0:T(128)}, u32[]{:S(2)}) copy-start(s32[128]{0:T(128)} %param.31) | copy-start | bytes 1540
  91.6 7.2 %copy-start.24 = (f32[720]{0:T(1024)S(1)}, f32[720]{0:T(1024)}, u32[]{:S(2)}) copy-start(f32[720]{0:T(1024)} %constant.97.clone) | copy-start | bytes 8644
  91.6 7.2 %copy-start.25 = (f32[720]{0:T(1024)S(1)}, f32[720]{0:T(1024)}, u32[]{:S(2)}) copy-start(f32[720]{0:T(1024)} %constant.98.clone) | copy-start | bytes 8644
  91.6 7.2 %copy-start.26 = (f32[720]{0:T(1024)S(1)}, f32[720]{0:T(1024)}, u32[]{:S(2)}) copy-start(f32[720]{0:T(1024)} %constant.99.clone) | copy-start | bytes 8644
  91.6 7.3 %copy-start.14 = (f32[45,720]{1,0:T(8,128)S(1)}, f32[45,720]{1,0:T(8,128)}, u32[]{:S(2)}) copy-start(f32[45,720]{1,0:T(8,128)} %constant.85.clone) | copy-start | bytes 388804
  91.6 7.3 %copy-start.15 = (f32[45,720]{1,0:T(8,128)S(1)}, f32[45,720]{1,0:T(8,128)}, u32[]{:S(2)}) copy-start(f32[45,720]{1,0:T(8,128)} %constant.86.clone) | copy-start | bytes 388804
  91.6 7.3 %copy-start.20 = (f32[16,720]{1,0:T(8,128)S(1)}, f32[16,720]{1,0:T(8,128)}, u32[]{:S(2)}) copy-start(f32[16,720]{1,0:T(8,128)} %constant.87.clone) | copy-start | bytes 138244
  91.6 7.3 %copy-start.21 = (f32[16,720]{1,0:T(8,128)S(1)}, f32[16,720]{1,0:T(8,128)}, u32[]{:S(2)}) copy-start(f32[16,720]{1,0:T(8,128)} %constant.88.clone) | copy-start | bytes 138244
  91.7 61.8 %all-to-all-start.1 = ((f32[4,12,16,720]{3,2,1,0:T(8,128)}), f32[4,12,16,720]{3,2,1,0:T(8,128)}, u32[]{:S(2)}, u32[]{:S(2)}) async-start(f32[4,12,16,720]{3,2,1,0:T(8,128)} %add.123), calls=%async_computation.1 | async-start | bytes 4718592 | tf_op jit(solution)/shard_map/all_to_all | solution.py:258
  98.7 1.0 copy-start.13
  98.7 1.0 copy-start.18
  98.7 1.0 copy-start.19
  99.0 2.5 copy-start.23
  99.0 2.6 copy-start.10
  99.0 2.6 copy-start.11
  99.0 2.6 copy-start.16
  99.0 2.6 copy-start.17
  155.2 6.4 %copy-start.6 = (f32[90,16,1440]{2,1,0:T(8,128)S(1)}, f32[90,16,1440]{2,1,0:T(8,128)}, u32[]{:S(2)}) copy-start(f32[90,16,1440]{2,1,0:T(8,128)} %multiply_subtract_fusion) | copy-start | bytes 24883204
  168.9 1.6 copy-start.7
  177.9 4.0 %copy-start.9 = (f32[24,16,720]{2,1,0:T(8,128)S(1)}, f32[24,16,720]{2,1,0:T(8,128)}, u32[]{:S(2)}) copy-start(f32[24,16,720]{2,1,0:T(8,128)} %param.30) | copy-start | bytes 3317764
  177.9 58.5 %all-to-all-start.2 = ((f32[4,12,16,720]{3,2,1,0:T(8,128)}), f32[4,12,16,720]{3,2,1,0:T(8,128)S(1)}, u32[]{:S(2)}, u32[]{:S(2)}) async-start(f32[4,12,16,720]{3,2,1,0:T(8,128)} %pad_maximum_fusion), calls=%async_computation.2 | async-start | bytes 4718592 | tf_op jit(solution)/shard_map/all_to_all | solution.py:293
  182.7 1.0 copy-start.8
  184.3 65.8 %collective-permute-start.5 = (f32[24,720]{1,0:T(8,128)}, f32[24,720]{1,0:T(8,128)}, u32[]{:S(2)}, u32[]{:S(2)}) collective-permute-start(f32[24,720]{1,0:T(8,128)} %slice_bitcast_fusion), channel_id=1, source_target_pairs={{0,4},{4,8},{8,12},{12,16},{16,20},{20,24},{24,28},{1,5},{5,9},{9,... | collective-permute-start | bytes 207368 | tf_op jit(solution)/shard_map/ppermute | solution.py:255
  188.2 57.4 %collective-permute-start.4 = (f32[24,16]{0,1:T(8,128)S(1)}, f32[24,16]{0,1:T(8,128)S(1)}, u32[]{:S(2)}, u32[]{:S(2)}) collective-permute-start(f32[24,16]{0,1:T(8,128)S(1)} %bitcast.109), channel_id=1, source_target_pairs={{0,1},{1,2},{2,3},{3,0},{4,5},{5,6},{6,7},{7,4},{8,9},{9,10},{10,1... | collective-permute-start | bytes 4616 | tf_op jit(solution)/shard_map/ppermute | solution.py:256
  237.3 17.8 %collective-permute-start.2 = (f32[2,24,720]{2,1,0:T(8,128)}, f32[2,24,720]{2,1,0:T(8,128)}, u32[]{:S(2)}, u32[]{:S(2)}) collective-permute-start(f32[2,24,720]{2,1,0:T(8,128)} %bitcast.83), channel_id=1, source_target_pairs={{4,0},{8,4},{12,8},{16,12},{20,16},{24,20},{28,24},{5,1},{9,5},{13... | collective-permute-start | bytes 414728 | tf_op jit(solution)/shard_map/ppermute | solution.py:296
  239.3 16.9 %collective-permute-start.3 = (f32[2,24,720]{2,1,0:T(8,128)}, f32[2,24,720]{2,1,0:T(8,128)}, u32[]{:S(2)}, u32[]{:S(2)}) collective-permute-start(f32[2,24,720]{2,1,0:T(8,128)} %bitcast.82), channel_id=1, source_target_pairs={{0,4},{4,8},{8,12},{12,16},{16,20},{20,24},{24,28},{1,5},{5,9},{9,... | collective-permute-start | bytes 414728 | tf_op jit(solution)/shard_map/ppermute | solution.py:297
  243.4 8.3 %collective-permute-start = (f32[2,24,16]{1,2,0:T(8,128)S(1)}, f32[2,24,16]{1,2,0:T(8,128)}, u32[]{:S(2)}, u32[]{:S(2)}) collective-permute-start(f32[2,24,16]{1,2,0:T(8,128)S(1)} %bitcast.106), channel_id=1, source_target_pairs={{1,0},{2,1},{3,2},{0,3},{5,4},{6,5},{7,6},{4,7},{9,8},{10,9},{11,1... | collective-permute-start | bytes 9224 | tf_op jit(solution)/shard_map/ppermute | solution.py:298
  246.2 7.2 %collective-permute-start.1 = (f32[2,24,16]{1,2,0:T(8,128)}, f32[2,24,16]{1,2,0:T(8,128)}, u32[]{:S(2)}, u32[]{:S(2)}) collective-permute-start(f32[2,24,16]{1,2,0:T(8,128)} %bitcast.30), channel_id=1, source_target_pairs={{0,1},{1,2},{2,3},{3,0},{4,5},{5,6},{6,7},{7,4},{8,9},{9,10},{10,1... | collective-permute-start | bytes 9224 | tf_op jit(solution)/shard_map/ppermute | solution.py:299
  257.2 1.3 copy-start.1
  258.4 1.0 copy-start.2
  259.4 1.0 copy-start.3
  (4 other events, 3.3 us)

commit v2 on v1

--- a/solution.py
+++ b/solution.py
@@ -114,58 +114,54 @@
     )(cells, values)
 
 
-def stencil_kernel(
-    field_ref, east_ref, north_ref, east_col, west_col, north_row, south_row,
-    wind_col, wind_row, out_ref, wide,
-):
+def stencil_kernel(keep_ref, field_ref, east_ref, north_ref, cols_ref, rows_ref, out_ref, wide, edge):
     tracers, levels, rows, width = field_ref.shape
     padded = wide.shape[1]
     lanes = lax.broadcasted_iota(jnp.int32, (rows, padded), 1)
     subs = lax.broadcasted_iota(jnp.int32, (rows, padded), 0)
+    keep = keep_ref[0]
 
     def widened(slot, block):
         wide[slot * rows : (slot + 1) * rows, 0:width] = block
         return wide[slot * rows : (slot + 1) * rows, :]
 
-    def wide_row(slot, block):
-        wide[slot * rows : slot * rows + 1, 0:width] = block
-        return wide[slot * rows : slot * rows + 1, :]
-
     for level in range(levels):
+        cols = cols_ref[level]
+        edge[0 : 2 * tracers + 1, 0:width] = rows_ref[level]
         wind_east = widened(0, east_ref[level])
-        wind_west = jnp.where(lanes == 0, wind_col[level], pltpu.roll(wind_east, 1, 1))
+        wind_west = jnp.where(
+            lanes == 0, cols[:, 2 * tracers : 2 * tracers + 1], pltpu.roll(wind_east, 1, 1)
+        )
         wind_north = widened(1, north_ref[level])
         wind_south = jnp.where(
-            subs == 0, wide_row(2, wind_row[level]), pltpu.roll(wind_north, 1, 0)
+            subs == 0, edge[2 * tracers : 2 * tracers + 1, :], pltpu.roll(wind_north, 1, 0)
         )
+        wind_north = jnp.where((subs == rows - 1) & (keep == 0), 0.0, wind_north)
         east_face = jnp.maximum(wind_east, 0.0)
         west_face = jnp.minimum(wind_west, 0.0)
         north_face = jnp.maximum(wind_north, 0.0)
         south_face = jnp.minimum(wind_south, 0.0)
         for tracer in range(tracers):
-            center = widened(3 + 3 * tracer, field_ref[tracer, level])
+            other = tracers + tracer
+            center = widened(2 + tracer, field_ref[tracer, level])
             east_val = jnp.where(
-                lanes == width - 1, east_col[tracer, level], pltpu.roll(center, padded - 1, 1)
+                lanes == width - 1, cols[:, tracer : tracer + 1], pltpu.roll(center, padded - 1, 1)
             )
-            west_val = jnp.where(lanes == 0, west_col[tracer, level], pltpu.roll(center, 1, 1))
+            west_val = jnp.where(lanes == 0, cols[:, other : other + 1], pltpu.roll(center, 1, 1))
             upper_val = jnp.where(
-                subs == rows - 1,
-                wide_row(4 + 3 * tracer, north_row[tracer, level]),
-                pltpu.roll(center, rows - 1, 0),
+                subs == rows - 1, edge[tracer : tracer + 1, :], pltpu.roll(center, rows - 1, 0)
             )
-            lower_val = jnp.where(
-                subs == 0,
-                wide_row(5 + 3 * tracer, south_row[tracer, level]),
-                pltpu.roll(center, 1, 0),
-            )
+            lower_val = jnp.where(subs == 0, edge[other : other + 1, :], pltpu.roll(center, 1, 0))
             result = center + east_face * (east_val - center) + west_face * (center - west_val)
             result = result + north_face * (upper_val - center) + south_face * (center - lower_val)
             out_ref[tracer, level] = result[:, 0:width]
 
 
-def advect(field, wind_east, wind_north, east_col, west_col, north_row, south_row, wind_col, wind_row):
+def advect(keep, field, wind_east, wind_north, cols, rows_edge):
     tracers, levels, rows, width = field.shape
     step = 4 if levels % 4 == 0 else 1
+    padded = -(-(width + 1) // 128) * 128
+    edges = 2 * tracers + 1
 
     def four(depth, span):
         return pl.BlockSpec((tracers, step, depth, span), lambda i: (0, i, 0, 0))
@@ -173,20 +169,22 @@
     def three(depth, span):
         return pl.BlockSpec((step, depth, span), lambda i: (i, 0, 0))
 
-    padded = -(-(width + 1) // 128) * 128
     return pl.pallas_call(
         stencil_kernel,
         grid=(levels // step,),
         out_shape=jax.ShapeDtypeStruct(field.shape, jnp.float32),
         in_specs=[
+            pl.BlockSpec(memory_space=pltpu.SMEM),
             four(rows, width), three(rows, width), three(rows, width),
-            four(rows, 1), four(rows, 1), four(1, width), four(1, width),
-            three(rows, 1), three(1, width),
+            three(rows, edges), three(edges, width),
         ],
         out_specs=four(rows, width),
-        scratch_shapes=[pltpu.VMEM(((3 + 3 * tracers) * rows, padded), jnp.float32)],
+        scratch_shapes=[
+            pltpu.VMEM(((2 + tracers) * rows, padded), jnp.float32),
+            pltpu.VMEM((8, padded), jnp.float32),
+        ],
         compiler_params=pltpu.CompilerParams(vmem_limit_bytes=32 * 1024 * 1024),
-    )(field, wind_east, wind_north, east_col, west_col, north_row, south_row, wind_col, wind_row)
+    )(keep, field, wind_east, wind_north, cols, rows_edge)
 
 
 def owner_positions(owner_dev, devices):
@@ -247,18 +245,31 @@
     )
 
     local_rows = lat_index * lat_dev + jnp.arange(lat_dev, dtype=jnp.int32)
-    north_wind = jnp.where(local_rows[None, :, None] < total_rows - 1, wind_north, 0.0)
     up = [(i, i + 1) for i in range(lat_count - 1)]
     down = [(i + 1, i) for i in range(lat_count - 1)]
     east = [(i, (i + 1) % lon_count) for i in range(lon_count)]
     west = [((i + 1) % lon_count, i) for i in range(lon_count)]
-    wind_row = lax.ppermute(north_wind[:, -1, :], "lat", up)[:, None, :]
-    wind_col = lax.ppermute(wind_east[:, :, -1], "lon", east)[:, :, None]
-
-    grouped = lax.all_to_all(
-        adjoint.reshape(lon_count, fields // lon_count, lat_dev, lon_dev),
-        "lon", split_axis=0, concat_axis=0, tiled=True,
-    )
+
+    caps = -(-(total_rows // 8) // lat_dev)
+    polar_bands = sorted(set(range(caps)) | set(range(lat_count - caps, lat_count)))
+    share = fields // lon_count
+    lon_index = lax.axis_index("lon")
+
+    def among_polar(block, shift):
+        pairs = [
+            (band * lon_count + z, band * lon_count + (z + shift) % lon_count)
+            for band in polar_bands
+            for z in range(lon_count)
+        ]
+        return lax.ppermute(block, ("lat", "lon"), pairs)
+
+    def own_share(array, shift):
+        start = (lon_index + shift) % lon_count * share
+        return lax.dynamic_slice_in_dim(array, start, share, axis=0)
+
+    grouped = [own_share(adjoint, 0)]
+    for m in range(1, lon_count):
+        grouped.append(among_polar(own_share(adjoint, -m), -m))
     lat_ratio = jnp.sin(math.pi * (local_rows.astype(jnp.float32) + 0.5) / total_rows) / math.sin(
         math.pi * (total_rows // 8) / total_rows
     )
@@ -277,29 +288,29 @@
     pair_part = filt(pair, *tables[2])
     first, second = pair_part[:, :, :quarter], pair_part[:, :, quarter:]
     even_part, odd_part = zero_part + two_part, zero_part - two_part
-    results = [
-        quarters[0] + (even_part + first),
-        quarters[1] + (odd_part + second),
-        quarters[2] + (even_part - first),
-        quarters[3] + (odd_part - second),
-    ]
-    filtered = jnp.stack(
-        [
-            result[:, :, j * lon_dev : (j + 1) * lon_dev]
-            for result in results
-            for j in range(blocks)
-        ]
-    )
-    field = lax.all_to_all(filtered, "lon", split_axis=0, concat_axis=0, tiled=True)
+    results = [even_part + first, odd_part + second, even_part - first, odd_part - second]
+    field = adjoint
+    for m in range(lon_count):
+        spot = (m % blocks) * lon_dev
+        change = results[m // blocks][:, :, spot : spot + lon_dev]
+        if m > 0:
+            change = among_polar(change, m)
+        start = (lon_index - m) % lon_count * share
+        field = lax.dynamic_update_slice_in_dim(field, own_share(adjoint, -m) + change, start, axis=0)
     field = field.reshape(tracers, levels, lat_dev, lon_dev)
 
-    north_row = lax.ppermute(field[:, :, 0, :], "lat", down)[:, :, None, :]
-    south_row = lax.ppermute(field[:, :, -1, :], "lat", up)[:, :, None, :]
-    east_col = lax.ppermute(field[:, :, :, 0], "lon", west)[..., None]
-    west_col = lax.ppermute(field[:, :, :, -1], "lon", east)[..., None]
-    return advect(
-        field, wind_east, north_wind, east_col, west_col, north_row, south_row, wind_col, wind_row
-    )
+    from_east = lax.ppermute(field[:, :, :, 0], "lon", west)
+    from_west = lax.ppermute(
+        jnp.concatenate([field[:, :, :, -1], wind_east[None, :, :, -1]]), "lon", east
+    )
+    from_north = lax.ppermute(field[:, :, 0, :], "lat", down)
+    from_south = lax.ppermute(
+        jnp.concatenate([field[:, :, -1, :], wind_north[None, :, -1, :]]), "lat", up
+    )
+    cols = jnp.concatenate([from_east, from_west]).transpose(1, 2, 0)
+    rows_edge = jnp.concatenate([from_north, from_south]).transpose(1, 0, 2)
+    keep = (lat_index < lat_count - 1).astype(jnp.int32).reshape(1)
+    return advect(keep, field, wind_east, wind_north, cols, rows_edge)
 
 
 def solution(mesh):

time: 268 us -> 203 us (0.76)
  waiting for transfers between devices: 93.4 us -> 56.9 us
  blocking collectives: 32.2 us -> 0 us
  starting transfers between devices: 22.4 us -> 41.3 us
  local copies, waits for them, and re-layouts: 53.1 us -> 40.6 us
  matrix products: 22.4 us -> 15.7 us
  Pallas kernels: 23.9 us -> 26.6 us
    all_to_all x2 -> x1, waiting for transfers between devices: 93.4 us -> 21.3 us  [shards(): lax.all_to_all(send.reshape(devices, capacity, 32), ('lat', 'lon'), split...]
    ppermute x6 -> x10, waiting for transfers between devices: 0.02 us -> 35.7 us  [the longest x6 34 us: among_polar(): return lax.ppermute(block, ('lat', 'lon'), pairs)]
    all_to_all x1 -> x0, blocking collectives: 32.2 us -> none  [shards(): lax.all_to_all(send.reshape(devices, capacity, 32), ('lat', 'lon'), split...]
    ppermute x6 -> x10, starting transfers between devices: 11.4 us -> 34 us  [the longest x6 22.5 us: among_polar(): return lax.ppermute(block, ('lat', 'lon'), pairs)]
    broadcast_in_dim x6 -> x0, local copies, waits for them, and re-layouts: 8.59 us -> none  [the longest x1 1.73 us: shards(): west_col = lax.ppermute(field[:, :, :, -1], 'lon', east)[..., None]]
    dot_general x3, matrix products: 11.8 us -> 5.86 us  [corrected(): jnp.dot(data.reshape(fields * rows, width), basis, precision=precise_mode)]
    transpose x1 -> x0, local copies, waits for them, and re-layouts: 5.6 us -> none  [shards(): forcing.T.reshape(fields, lat_dev, lon_dev)]
    unnamed x59 -> x54, local copies, waits for them, and re-layouts: 11.2 us -> 7.16 us
  transfers between devices with their start and end apart: 8 -> 11, of which waited for: 2 -> 6; matrix products, arithmetic and copies ran while one was open for 8% -> 10% of each run, Pallas kernels for 0% -> 0%
where the time goes in v2:
time: 203 us; the launch traced here: 202 us
  waiting for transfers between devices  56.9 us (28%)
  starting transfers between devices  41.3 us (20%)
  local copies, waits for them, and re-layouts  40.6 us (20%)
  Pallas kernels  26.6 us (13%)
  other arithmetic  20 us (10%)
  matrix products  15.7 us (8%)
    ppermute x6, waiting for transfers between devices, among_polar(): return lax.ppermute(block, ('lat', 'lon'), pairs)  34 us
    ppermute x6, starting transfers between devices, among_polar(): return lax.ppermute(block, ('lat', 'lon'), pairs)  22.5 us
    pallas_call x1, Pallas kernels, add_soundings(): pl.pallas_call(scatter_kernel, out_shape=jax.ShapeDtypeStruct((total, wid...  22.3 us
    all_to_all x1, waiting for transfers between devices, shards(): lax.all_to_all(send.reshape(devices, capacity, 32), ('lat', 'lon'), split...  21.3 us
    scatter x1, local copies, waits for them, and re-layouts, shards(): jnp.zeros((devices * capacity, 32), jnp.float32).at[slot_index]  12.8 us
    dot_general x3, matrix products, corrected(): lax.dot_general(spectra, basis, (((1,), (1,)), ((), ())), precision=preci...  8.01 us
    all_to_all x1, starting transfers between devices, shards(): lax.all_to_all(send.reshape(devices, capacity, 32), ('lat', 'lon'), split...  7.3 us
    unnamed x54, local copies, waits for them, and re-layouts  7.16 us
  transfers between devices with their start and end apart: 11, of which 6 were waited for; matrix products, arithmetic and copies ran while one was open for 10% of the time, Pallas kernels for 0%

profile of v2, /device:TPU:0, one launch (start us, length us, event | category | flops | bytes accessed | tf_op | source)
XLA Modules:
  0.0 201.9 jit_solution(12813206556794113245)
XLA Ops:
  6.5 12.8 %scatter_custom_fusion = f32[8192,32]{1,0:T(8,128)} fusion(s32[4096]{0:T(1024)S(1)} %bitcast.79, f32[4096,32]{1,0:T(8,128)S(1)} %copy.55, f32[]{:T(128)} %constant.123.clone.1), kind=kCustom, calls=%fused_computation.6 | custom fusion | bytes 1048580 | tf_op jit(solution)/shard_map/scatter | solution.py:231
  19.3 3.6 %copy.56 = f32[32,256,32]{1,2,0:T(8,128)} copy(f32[32,256,32]{2,1,0:T(8,128)} %bitcast.66) | data formatting | bytes 2097152 | tf_op jit(solution)/shard_map/reshape | solution.py:235
  23.0 7.3 %all-to-all-start = ((f32[32,256,32]{1,2,0:T(8,128)}), f32[32,256,32]{1,2,0:T(8,128)S(1)}, u32[]{:S(2)}, u32[]{:S(2)}) async-start(f32[32,256,32]{1,2,0:T(8,128)} %copy.56), calls=%async_computation | async-start | bytes 2097152 | tf_op jit(solution)/shard_map/all_to_all | solution.py:234
  30.5 1.7 multiply_subtract_fusion.2
  32.3 1.8 multiply_subtract_fusion.1
  34.1 21.3 %all-to-all-done = f32[32,256,32]{1,2,0:T(8,128)S(1)} async-done(((f32[32,256,32]{1,2,0:T(8,128)}), f32[32,256,32]{1,2,0:T(8,128)S(1)}, u32[]{:S(2)}, u32[]{:S(2)}) %all-to-all-start) | async-done | bytes 1048608 | tf_op jit(solution)/shard_map/all_to_all | solution.py:234
  55.7 2.7 %copy.58.values_ref = f32[8192,48]{1,0:T(8,128)} copy(f32[8192,48]{0,1:T(8,128)S(1)} %bitcast.67) | data formatting | bytes 3145728 | tf_op jit(solution)/shard_map/mul | solution.py:239
  58.4 2.2 %copy-done = f32[8192,48]{1,0:T(8,128)S(1)} copy-done((f32[8192,48]{1,0:T(8,128)S(1)}, f32[8192,48]{1,0:T(8,128)}, u32[]{:S(2)}) %copy-start) | copy-done | bytes 1572888
  60.6 22.3 %shard_map.262 = f32[11520,48]{1,0:T(8,128)} custom-call(s32[8192]{0:T(1024)S(1)} %bitcast.58, f32[8192,48]{1,0:T(8,128)S(1)} %copy-done), custom_call_target="tpu_custom_call" | custom-call | tf_op jit(solution)/shard_map/pallas_call | solution.py:104
  82.9 4.6 %copy.59 = f32[48,16,720]{2,1,0:T(8,128)S(1)} copy(f32[48,16,720]{0,2,1:T(8,128)} %bitcast.61) | data formatting | bytes 4423680 | tf_op jit(solution)/shard_map/reshape | solution.py:244
  87.6 2.1 %bitcast_add_fusion = f32[48,16,720]{2,1,0:T(8,128)S(1)} fusion(f32[48,16,720]{2,1,0:T(8,128)S(1)} %copy.59, f32[2,24,16,720]{3,2,1,0:T(8,128)} %param.28), kind=kLoop, calls=%fused_computation.3 | loop fusion | flops 552960 | bytes 6635520 | tf_op jit(solution)/shard_map/add | solution.py:243
  89.8 4.2 %collective-permute-start = (f32[12,16,720]{2,1,0:T(8,128)S(1)}, f32[12,16,720]{2,1,0:T(8,128)S(1)}, u32[]{:S(2)}, u32[]{:S(2)}) collective-permute-start(f32[12,16,720]{2,1,0:T(8,128)S(1)} %constant_dynamic-slice_fusion.2), channel_id=1, source_target_pairs={{0,2},{1,3},{2,0},{3,1},{28,30},{29,31},{30,28},{31,29}} | collective-permute-start | bytes 1658888 | tf_op jit(solution)/shard_map/ppermute | solution.py:264
  95.6 13.1 %collective-permute-done = f32[12,16,720]{2,1,0:T(8,128)S(1)} collective-permute-done((f32[12,16,720]{2,1,0:T(8,128)S(1)}, f32[12,16,720]{2,1,0:T(8,128)S(1)}, u32[]{:S(2)}, u32[]{:S(2)}) %collective-permute-start) | collective-permute-done | bytes 552992 | tf_op jit(solution)/shard_map/ppermute | solution.py:264
  108.9 4.4 %collective-permute-start.1 = (f32[12,16,720]{2,1,0:T(8,128)S(1)}, f32[12,16,720]{2,1,0:T(8,128)S(1)}, u32[]{:S(2)}, u32[]{:S(2)}) collective-permute-start(f32[12,16,720]{2,1,0:T(8,128)S(1)} %get-tuple-element.39), channel_id=1, source_target_pairs={{0,3},{1,0},{2,1},{3,2},{28,31},{29,28},{30,29},{31,30}} | collective-permute-start | bytes 1658888 | tf_op jit(solution)/shard_map/ppermute | solution.py:264
  113.2 2.1 %collective-permute-start.2 = (f32[12,16,720]{2,1,0:T(8,128)S(1)}, f32[12,16,720]{2,1,0:T(8,128)S(1)}, u32[]{:S(2)}, u32[]{:S(2)}) collective-permute-start(f32[12,16,720]{2,1,0:T(8,128)S(1)} %get-tuple-element.38), channel_id=1, source_target_pairs={{0,1},{1,2},{2,3},{3,0},{28,29},{29,30},{30,31},{31,28}} | collective-permute-start | bytes 1658888 | tf_op jit(solution)/shard_map/ppermute | solution.py:264
  115.8 4.9 %collective-permute-done.1 = f32[12,16,720]{2,1,0:T(8,128)S(1)} collective-permute-done((f32[12,16,720]{2,1,0:T(8,128)S(1)}, f32[12,16,720]{2,1,0:T(8,128)S(1)}, u32[]{:S(2)}, u32[]{:S(2)}) %collective-permute-start.1) | collective-permute-done | bytes 552992 | tf_op jit(solution)/shard_map/ppermute | solution.py:264
  120.7 6.7 %collective-permute-done.2 = f32[12,16,720]{2,1,0:T(8,128)S(1)} collective-permute-done((f32[12,16,720]{2,1,0:T(8,128)S(1)}, f32[12,16,720]{2,1,0:T(8,128)S(1)}, u32[]{:S(2)}, u32[]{:S(2)}) %collective-permute-start.2) | collective-permute-done | bytes 552992 | tf_op jit(solution)/shard_map/ppermute | solution.py:264
  129.9 3.5 %convolution_multiply_fusion = f32[12,16,1440]{2,1,0:T(8,128)S(1)} fusion(f32[1440,1440,1]{1,0,2:T(8,128)S(1)} %bitcast.59, f32[12,16,720]{2,1,0:T(8,128)S(1)} %sub.77, f32[12,16,720]{2,1,0:T(8,128)S(1)} %get-tuple-element.37, f32[16,1440]{1,0:T(8,128)S(1)} %multiply_select_fusion), kind=kOutput, calls=%fused_computation.2 | convolution fusion | flops 2389340160 | bytes 10598400 | tf_op jit(solution)/shard_map/dot_general | solution.py:53
  133.4 4.3 %fusion.18 = f32[12,16,1440]{2,1,0:T(8,128)S(1)} fusion(f32[12,16,1440]{2,1,0:T(8,128)S(1)} %convolution_multiply_fusion, f32[1440,1440,1]{1,0,2:T(8,128)S(1)} %bitcast.60), kind=kOutput, calls=%fused_computation.59 | convolution fusion | flops 2388787200 | bytes 10506240 | tf_op jit(solution)/shard_map/dot_general | solution.py:55
  138.9 2.5 %slice_subtract_fusion = (f32[12,16,720]{2,1,0:T(8,128)}, f32[12,16,720]{2,1,0:T(8,128)}, f32[12,16,720]{2,1,0:T(8,128)}, f32[48,16,720]{2,1,0:T(8,128)S(1)}) fusion(f32[12,16,1440]{2,1,0:T(8,128)S(1)} %fusion.18, f32[12,16,720]{2,1,0:T(8,128)S(1)} %fusion.17, f32[48,16,720]{2,1,0:T(8,128)S(1)} %copy.74, s32[]{:T(128)S(6)} %select_n.87, ...), kind=kOutput, calls=%fused_computation.22 | convolution fusion | flops 598164480 | bytes 7409668 | tf_op jit(solution)/shard_map/dot_general | solution.py:55
  141.4 4.0 %collective-permute-start.3 = (f32[12,16,720]{2,1,0:T(8,128)}, f32[12,16,720]{2,1,0:T(8,128)}, u32[]{:S(2)}, u32[]{:S(2)}) collective-permute-start(f32[12,16,720]{2,1,0:T(8,128)} %get-tuple-element.35), channel_id=1, source_target_pairs={{0,1},{1,2},{2,3},{3,0},{28,29},{29,30},{30,31},{31,28}} | collective-permute-start | bytes 1658888 | tf_op jit(solution)/shard_map/ppermute | solution.py:264
  145.4 4.5 %collective-permute-start.4 = (f32[12,16,720]{2,1,0:T(8,128)}, f32[12,16,720]{2,1,0:T(8,128)}, u32[]{:S(2)}, u32[]{:S(2)}) collective-permute-start(f32[12,16,720]{2,1,0:T(8,128)} %get-tuple-element.34), channel_id=1, source_target_pairs={{0,2},{1,3},{2,0},{3,1},{28,30},{29,31},{30,28},{31,29}} | collective-permute-start | bytes 1658888 | tf_op jit(solution)/shard_map/ppermute | solution.py:264
  149.9 3.4 %collective-permute-start.5 = (f32[12,16,720]{2,1,0:T(8,128)}, f32[12,16,720]{2,1,0:T(8,128)}, u32[]{:S(2)}, u32[]{:S(2)}) collective-permute-start(f32[12,16,720]{2,1,0:T(8,128)} %get-tuple-element.33), channel_id=1, source_target_pairs={{0,3},{1,0},{2,1},{3,2},{28,31},{29,28},{30,29},{31,30}} | collective-permute-start | bytes 1658888 | tf_op jit(solution)/shard_map/ppermute | solution.py:264
  153.2 1.8 slice_bitcast_fusion
  155.8 1.7 copy.66
  158.8 9.3 %collective-permute-done.4 = f32[12,16,720]{2,1,0:T(8,128)} collective-permute-done((f32[12,16,720]{2,1,0:T(8,128)}, f32[12,16,720]{2,1,0:T(8,128)}, u32[]{:S(2)}, u32[]{:S(2)}) %collective-permute-start.4) | collective-permute-done | bytes 552992 | tf_op jit(solution)/shard_map/ppermute | solution.py:264
  172.9 2.0 collective-permute-start.9
  179.5 5.5 %collective-permute-start.7 = (f32[3,24,16]{1,2,0:T(8,128)}, f32[3,24,16]{1,2,0:T(8,128)}, u32[]{:S(2)}, u32[]{:S(2)}) collective-permute-start(f32[3,24,16]{1,2,0:T(8,128)} %pad_maximum_fusion.2), channel_id=1, source_target_pairs={{0,1},{1,2},{2,3},{3,0},{4,5},{5,6},{6,7},{7,4},{8,9},{9,10},{10,1... | collective-permute-start | bytes 13832 | tf_op jit(solution)/shard_map/ppermute | solution.py:303
  185.0 1.9 copy.60
  186.8 2.8 %collective-permute-start.6 = (f32[2,24,16]{1,2,0:T(8,128)}, f32[2,24,16]{1,2,0:T(8,128)S(1)}, u32[]{:S(2)}, u32[]{:S(2)}) collective-permute-start(f32[2,24,16]{1,2,0:T(8,128)} %bitcast.80), channel_id=1, source_target_pairs={{1,0},{2,1},{3,2},{0,3},{5,4},{6,5},{7,6},{4,7},{9,8},{10,9},{11,1... | collective-permute-start | bytes 9224 | tf_op jit(solution)/shard_map/ppermute | solution.py:302
  189.6 1.7 collective-permute-done.6
  197.6 4.3 %shard_map.263 = f32[2,24,16,720]{3,2,1,0:T(8,128)} custom-call(s32[1]{0:T(128)} %bitcast.keep_ref, f32[2,24,16,720]{3,2,1,0:T(8,128)S(1)} %bitcast.56, f32[24,16,720]{2,1,0:T(8,128)S(1)} %copy-done.1, f32[24,16,720]{2,1,0:T(8,128)S(1)} %copy-done.2, f32[24,16,5]{2,1,0:T(8,128)S(1)} %bitcast.57, f32[24,5,720]{2,1,0:T(8,128)S(1)} %maximum_bitcast_fusion.rows_ref), custom_call_target="tpu_custom_call" | custom-call | tf_op jit(solution)/shard_map/pallas_call | solution.py:172
  (97 shorter events, 30.5 us)
Async XLA Ops:
  22.9 7.5 %copy-start.24 = (s32[128]{0:T(128)S(1)}, s32[128]{0:T(128)}, u32[]{:S(2)}) copy-start(s32[128]{0:T(128)} %param.31) | copy-start | bytes 1540
  22.9 7.6 %copy-start.12 = (f32[45,720]{1,0:T(8,128)S(1)}, f32[45,720]{1,0:T(8,128)}, u32[]{:S(2)}) copy-start(f32[45,720]{1,0:T(8,128)} %constant.143.clone) | copy-start | bytes 388804
  22.9 7.6 %copy-start.13 = (f32[45,720]{1,0:T(8,128)S(1)}, f32[45,720]{1,0:T(8,128)}, u32[]{:S(2)}) copy-start(f32[45,720]{1,0:T(8,128)} %constant.144.clone) | copy-start | bytes 388804
  22.9 7.6 %copy-start.18 = (f32[16,720]{1,0:T(8,128)S(1)}, f32[16,720]{1,0:T(8,128)}, u32[]{:S(2)}) copy-start(f32[16,720]{1,0:T(8,128)} %constant.145.clone) | copy-start | bytes 138244
  22.9 7.6 %copy-start.19 = (f32[16,720]{1,0:T(8,128)S(1)}, f32[16,720]{1,0:T(8,128)}, u32[]{:S(2)}) copy-start(f32[16,720]{1,0:T(8,128)} %constant.146.clone) | copy-start | bytes 138244
  22.9 9.4 %copy-start.10 = (f32[45,720]{1,0:T(8,128)S(1)}, f32[45,720]{1,0:T(8,128)}, u32[]{:S(2)}) copy-start(f32[45,720]{1,0:T(8,128)} %constant.147.clone) | copy-start | bytes 388804
  22.9 9.3 %copy-start.11 = (f32[45,720]{1,0:T(8,128)S(1)}, f32[45,720]{1,0:T(8,128)}, u32[]{:S(2)}) copy-start(f32[45,720]{1,0:T(8,128)} %constant.148.clone) | copy-start | bytes 388804
  23.0 9.3 %copy-start.16 = (f32[16,720]{1,0:T(8,128)S(1)}, f32[16,720]{1,0:T(8,128)}, u32[]{:S(2)}) copy-start(f32[16,720]{1,0:T(8,128)} %constant.149.clone) | copy-start | bytes 138244
  23.0 9.3 %copy-start.17 = (f32[16,720]{1,0:T(8,128)S(1)}, f32[16,720]{1,0:T(8,128)}, u32[]{:S(2)}) copy-start(f32[16,720]{1,0:T(8,128)} %constant.150.clone) | copy-start | bytes 138244
  23.0 32.4 %all-to-all-start = ((f32[32,256,32]{1,2,0:T(8,128)}), f32[32,256,32]{1,2,0:T(8,128)S(1)}, u32[]{:S(2)}, u32[]{:S(2)}) async-start(f32[32,256,32]{1,2,0:T(8,128)} %copy.56), calls=%async_computation | async-start | bytes 2097152 | tf_op jit(solution)/shard_map/all_to_all | solution.py:234
  87.5 6.5 %copy-start.7 = (f32[90,1440]{1,0:T(8,128)S(1)}, f32[90,1440]{1,0:T(8,128)}, u32[]{:S(2)}) copy-start(f32[90,1440]{1,0:T(8,128)} %constant.151.clone) | copy-start | bytes 1555204
  87.5 6.5 %copy-start.8 = (f32[90,1440]{1,0:T(8,128)S(1)}, f32[90,1440]{1,0:T(8,128)}, u32[]{:S(2)}) copy-start(f32[90,1440]{1,0:T(8,128)} %constant.152.clone) | copy-start | bytes 1555204
  87.5 6.5 %copy-start.14 = (f32[16,1440]{1,0:T(8,128)S(1)}, f32[16,1440]{1,0:T(8,128)}, u32[]{:S(2)}) copy-start(f32[16,1440]{1,0:T(8,128)} %constant.153.clone) | copy-start | bytes 276484
  87.5 6.5 %copy-start.15 = (f32[16,1440]{1,0:T(8,128)S(1)}, f32[16,1440]{1,0:T(8,128)}, u32[]{:S(2)}) copy-start(f32[16,1440]{1,0:T(8,128)} %constant.154.clone) | copy-start | bytes 276484
  89.7 48.0 %copy-start.4 = (f32[48,16,720]{2,1,0:T(8,128)}, f32[48,16,720]{2,1,0:T(8,128)S(1)}, u32[]{:S(2)}) copy-start(f32[48,16,720]{2,1,0:T(8,128)S(1)} %bitcast_add_fusion) | copy-start | bytes 6635524
  89.8 18.9 %collective-permute-start = (f32[12,16,720]{2,1,0:T(8,128)S(1)}, f32[12,16,720]{2,1,0:T(8,128)S(1)}, u32[]{:S(2)}, u32[]{:S(2)}) collective-permute-start(f32[12,16,720]{2,1,0:T(8,128)S(1)} %constant_dynamic-slice_fusion.2), channel_id=1, source_target_pairs={{0,2},{1,3},{2,0},{3,1},{28,30},{29,31},{30,28},{31,29}} | collective-permute-start | bytes 1658888 | tf_op jit(solution)/shard_map/ppermute | solution.py:264
  95.6 19.8 %copy-start.21 = (f32[720]{0:T(1024)S(1)}, f32[720]{0:T(1024)}, u32[]{:S(2)}) copy-start(f32[720]{0:T(1024)} %constant.155.clone) | copy-start | bytes 8644
  95.6 19.8 %copy-start.22 = (f32[720]{0:T(1024)S(1)}, f32[720]{0:T(1024)}, u32[]{:S(2)}) copy-start(f32[720]{0:T(1024)} %constant.156.clone) | copy-start | bytes 8644
  95.6 19.8 %copy-start.23 = (f32[720]{0:T(1024)S(1)}, f32[720]{0:T(1024)}, u32[]{:S(2)}) copy-start(f32[720]{0:T(1024)} %constant.157.clone) | copy-start | bytes 8644
  95.6 19.9 %copy-start.20 = (f32[1440]{0:T(1024)S(1)}, f32[1440]{0:T(1024)}, u32[]{:S(2)}) copy-start(f32[1440]{0:T(1024)} %constant.159.clone) | copy-start | bytes 17284
  108.9 11.8 %collective-permute-start.1 = (f32[12,16,720]{2,1,0:T(8,128)S(1)}, f32[12,16,720]{2,1,0:T(8,128)S(1)}, u32[]{:S(2)}, u32[]{:S(2)}) collective-permute-start(f32[12,16,720]{2,1,0:T(8,128)S(1)} %get-tuple-element.39), channel_id=1, source_target_pairs={{0,3},{1,0},{2,1},{3,2},{28,31},{29,28},{30,29},{31,30}} | collective-permute-start | bytes 1658888 | tf_op jit(solution)/shard_map/ppermute | solution.py:264
  113.2 14.2 %collective-permute-start.2 = (f32[12,16,720]{2,1,0:T(8,128)S(1)}, f32[12,16,720]{2,1,0:T(8,128)S(1)}, u32[]{:S(2)}, u32[]{:S(2)}) collective-permute-start(f32[12,16,720]{2,1,0:T(8,128)S(1)} %get-tuple-element.38), channel_id=1, source_target_pairs={{0,1},{1,2},{2,3},{3,0},{28,29},{29,30},{30,31},{31,28}} | collective-permute-start | bytes 1658888 | tf_op jit(solution)/shard_map/ppermute | solution.py:264
  115.6 11.8 %copy-start.5 = (f32[45,16,720]{2,1,0:T(8,128)S(1)}, f32[45,16,720]{2,1,0:T(8,128)}, u32[]{:S(2)}) copy-start(f32[45,16,720]{2,1,0:T(8,128)} %multiply_subtract_fusion.1) | copy-start | bytes 6220804
  133.4 4.4 %copy-start.6 = (f32[45,16,720]{2,1,0:T(8,128)S(1)}, f32[45,16,720]{2,1,0:T(8,128)}, u32[]{:S(2)}) copy-start(f32[45,16,720]{2,1,0:T(8,128)} %multiply_subtract_fusion.2) | copy-start | bytes 6220804
  138.9 16.1 %copy-start.1 = (f32[24,16,720]{2,1,0:T(8,128)S(1)}, f32[24,16,720]{2,1,0:T(8,128)}, u32[]{:S(2)}) copy-start(f32[24,16,720]{2,1,0:T(8,128)} %east_ref.1) | copy-start | bytes 3317764
  141.4 16.0 %collective-permute-start.3 = (f32[12,16,720]{2,1,0:T(8,128)}, f32[12,16,720]{2,1,0:T(8,128)}, u32[]{:S(2)}, u32[]{:S(2)}) collective-permute-start(f32[12,16,720]{2,1,0:T(8,128)} %get-tuple-element.35), channel_id=1, source_target_pairs={{0,1},{1,2},{2,3},{3,0},{28,29},{29,30},{30,31},{31,28}} | collective-permute-start | bytes 1658888 | tf_op jit(solution)/shard_map/ppermute | solution.py:264
  145.4 22.7 %collective-permute-start.4 = (f32[12,16,720]{2,1,0:T(8,128)}, f32[12,16,720]{2,1,0:T(8,128)}, u32[]{:S(2)}, u32[]{:S(2)}) collective-permute-start(f32[12,16,720]{2,1,0:T(8,128)} %get-tuple-element.34), channel_id=1, source_target_pairs={{0,2},{1,3},{2,0},{3,1},{28,30},{29,31},{30,28},{31,29}} | collective-permute-start | bytes 1658888 | tf_op jit(solution)/shard_map/ppermute | solution.py:264
  149.9 19.5 %collective-permute-start.5 = (f32[12,16,720]{2,1,0:T(8,128)}, f32[12,16,720]{2,1,0:T(8,128)}, u32[]{:S(2)}, u32[]{:S(2)}) collective-permute-start(f32[12,16,720]{2,1,0:T(8,128)} %get-tuple-element.33), channel_id=1, source_target_pairs={{0,3},{1,0},{2,1},{3,2},{28,31},{29,28},{30,29},{31,30}} | collective-permute-start | bytes 1658888 | tf_op jit(solution)/shard_map/ppermute | solution.py:264
  172.9 21.3 %collective-permute-start.9 = (f32[3,24,720]{2,0,1:T(4,128)}, f32[3,24,720]{2,0,1:T(4,128)}, u32[]{:S(2)}, u32[]{:S(2)}) collective-permute-start(f32[3,24,720]{2,0,1:T(4,128)} %pad_maximum_fusion), channel_id=1, source_target_pairs={{0,4},{4,8},{8,12},{12,16},{16,20},{20,24},{24,28},{1,5},{5,9},{9,... | collective-permute-start | bytes 622088 | tf_op jit(solution)/shard_map/ppermute | solution.py:307
  175.7 18.6 %collective-permute-start.8 = (f32[2,24,720]{2,0,1:T(2,128)}, f32[2,24,720]{2,0,1:T(2,128)}, u32[]{:S(2)}, u32[]{:S(2)}) collective-permute-start(f32[2,24,720]{2,0,1:T(2,128)} %bitcast.53), channel_id=1, source_target_pairs={{4,0},{8,4},{12,8},{16,12},{20,16},{24,20},{28,24},{5,1},{9,5},{13... | collective-permute-start | bytes 414728 | tf_op jit(solution)/shard_map/ppermute | solution.py:306
  179.5 11.7 %collective-permute-start.7 = (f32[3,24,16]{1,2,0:T(8,128)}, f32[3,24,16]{1,2,0:T(8,128)}, u32[]{:S(2)}, u32[]{:S(2)}) collective-permute-start(f32[3,24,16]{1,2,0:T(8,128)} %pad_maximum_fusion.2), channel_id=1, source_target_pairs={{0,1},{1,2},{2,3},{3,0},{4,5},{5,6},{6,7},{7,4},{8,9},{9,10},{10,1... | collective-permute-start | bytes 13832 | tf_op jit(solution)/shard_map/ppermute | solution.py:303
  186.8 4.4 %collective-permute-start.6 = (f32[2,24,16]{1,2,0:T(8,128)}, f32[2,24,16]{1,2,0:T(8,128)S(1)}, u32[]{:S(2)}, u32[]{:S(2)}) collective-permute-start(f32[2,24,16]{1,2,0:T(8,128)} %bitcast.80), channel_id=1, source_target_pairs={{1,0},{2,1},{3,2},{0,3},{5,4},{6,5},{7,6},{4,7},{9,8},{10,9},{11,1... | collective-permute-start | bytes 9224 | tf_op jit(solution)/shard_map/ppermute | solution.py:302
  (4 other events, 7.0 us)

commit v3 on v2

--- a/solution.py
+++ b/solution.py
@@ -11,7 +11,7 @@
 
 precise_mode = lax.Precision.HIGH
 ACCS = 4
-UNROLL = 4
+UNROLL = 2
 
 
 def circle_tables(lon_width):
@@ -69,21 +69,24 @@
         return carry
 
     lax.fori_loop(0, total // chunk, clear, 0)
-    step = ACCS * UNROLL
+    step = 2 * ACCS * UNROLL
 
     def add(i, carry):
         base = i * step
         for turn in range(UNROLL):
-            places, olds = [], []
-            for lane in range(ACCS):
-                place = cells_ref[base + turn * ACCS + lane]
+            places, news = [], []
+            for lane in range(2 * ACCS):
+                spot = base + turn * 2 * ACCS + lane
+                acc = accs[lane % ACCS]
+                place = cells_ref[spot]
+                value = values_ref[pl.ds(spot, 1), :]
+                if lane >= ACCS:
+                    same = jnp.where(place == places[lane - ACCS], 1.0, 0.0)
+                    value = value + values_ref[pl.ds(spot - ACCS, 1), :] * same
                 places.append(place)
-                olds.append(
-                    accs[lane][pl.ds(place, 1), :]
-                    + values_ref[pl.ds(base + turn * ACCS + lane, 1), :]
-                )
-            for lane in range(ACCS):
-                accs[lane][pl.ds(places[lane], 1), :] = olds[lane]
+                news.append(acc[pl.ds(place, 1), :] + value)
+            for lane in range(2 * ACCS):
+                accs[lane % ACCS][pl.ds(places[lane], 1), :] = news[lane]
         return carry
 
     lax.fori_loop(0, count // step, add, 0)
@@ -97,6 +100,40 @@
         return carry
 
     lax.fori_loop(0, total // chunk, join, 0)
+
+
+def place_kernel(slots_ref, payload_ref, out_ref):
+    chunk = 64
+
+    def clear(i, carry):
+        where = pl.ds(pl.multiple_of(i * chunk, chunk), chunk)
+        out_ref[where, :] = jnp.zeros((chunk, out_ref.shape[1]), jnp.float32)
+        return carry
+
+    lax.fori_loop(0, out_ref.shape[0] // chunk, clear, 0)
+
+    def put(i, carry):
+        base = i * 16
+        rows = [payload_ref[pl.ds(base + j, 1), :] for j in range(16)]
+        slots = [slots_ref[base + j] for j in range(16)]
+        for slot, row in zip(slots, rows):
+            out_ref[pl.ds(slot, 1), :] = row
+        return carry
+
+    lax.fori_loop(0, payload_ref.shape[0] // 16, put, 0)
+
+
+def place_soundings(slots, payload, total):
+    return pl.pallas_call(
+        place_kernel,
+        out_shape=jax.ShapeDtypeStruct((total, payload.shape[1]), jnp.float32),
+        in_specs=[
+            pl.BlockSpec(memory_space=pltpu.SMEM),
+            pl.BlockSpec(memory_space=pltpu.VMEM),
+        ],
+        out_specs=pl.BlockSpec(memory_space=pltpu.VMEM),
+        compiler_params=pltpu.CompilerParams(vmem_limit_bytes=32 * 1024 * 1024),
+    )(slots, payload)
 
 
 def add_soundings(cells, values, total):
@@ -228,12 +265,13 @@
         ],
         axis=1,
     )
-    send = jnp.zeros((devices * capacity, 32), jnp.float32).at[slot_index].set(
-        payload, unique_indices=True
-    )
+    send = place_soundings(slot_index, payload, devices * capacity)
     got = lax.all_to_all(
         send.reshape(devices, capacity, 32), ("lat", "lon"), split_axis=0, concat_axis=0, tiled=True
     ).reshape(devices * capacity, 32)
+    tables = circle_tables(lon_width)
+    got, bases = lax.optimization_barrier((got, [table[0] for table in tables]))
+    tables = [(basis,) + table[1:] for basis, table in zip(bases, tables)]
     got_cells = got[:, levels + tracers].astype(jnp.int32)
     got_values = (
         got[:, levels : levels + tracers, None] * got[:, None, :levels]
@@ -267,14 +305,12 @@
         start = (lon_index + shift) % lon_count * share
         return lax.dynamic_slice_in_dim(array, start, share, axis=0)
 
-    grouped = [own_share(adjoint, 0)]
-    for m in range(1, lon_count):
-        grouped.append(among_polar(own_share(adjoint, -m), -m))
+    shares = lax.optimization_barrier([own_share(adjoint, -m) for m in range(lon_count)])
+    grouped = [among_polar(block, -m) if m else block for m, block in enumerate(shares)]
     lat_ratio = jnp.sin(math.pi * (local_rows.astype(jnp.float32) + 0.5) / total_rows) / math.sin(
         math.pi * (total_rows // 8) / total_rows
     )
     live = lax.dynamic_slice_in_dim(polar_mask, lat_index * lat_dev, lat_dev) > 0
-    tables = circle_tables(lon_width)
     blocks = lon_count // 4
     quarters = [
         jnp.concatenate([grouped[blocks * i + j] for j in range(blocks)], axis=2) for i in range(4)

time: 203 us -> 198 us (0.975)
  local copies, waits for them, and re-layouts: 40.6 us -> 33 us
  starting transfers between devices: 41.3 us -> 36.9 us
  Pallas kernels: 26.6 us -> 30.9 us
  other arithmetic: 20 us -> 24.2 us
  waiting for transfers between devices: 56.9 us -> 54.1 us
    scatter x1 -> x0, local copies, waits for them, and re-layouts: 12.8 us -> none  [shards(): jnp.zeros((devices * capacity, 32), jnp.float32).at[slot_index]]
    pallas_call x0 -> x1, Pallas kernels: none -> 5.85 us  [place_soundings(): pl.pallas_call(place_kernel, out_shape=jax.ShapeDtypeStruct((total, paylo...]
    all_to_all x1, waiting for transfers between devices: 21.3 us -> 16.4 us  [shards(): lax.all_to_all(send.reshape(devices, capacity, 32), ('lat', 'lon'), split...]
    unnamed x54 -> x60, local copies, waits for them, and re-layouts: 7.16 us -> 11.4 us
    sub x3, other arithmetic: 5.02 us -> 8.38 us  [table(): full = cos_high[:, None] * cos_low[None] - sin_high[:, None] * sin_low[None]]
    ppermute x1, starting transfers between devices: 2.77 us -> 0.01 us  [shards(): from_east = lax.ppermute(field[:, :, :, 0], 'lon', west)]
    ppermute x1, waiting for transfers between devices: 1.65 us -> 4 us  [shards(): from_east = lax.ppermute(field[:, :, :, 0], 'lon', west)]
  transfers between devices with their start and end apart: 11 -> 11, of which waited for: 6 -> 7; matrix products, arithmetic and copies ran while one was open for 10% -> 12% of each run, Pallas kernels for 0% -> 0%
where the time goes in v3:
time: 198 us; the launch traced here: 196 us
  waiting for transfers between devices  54.1 us (27%)
  starting transfers between devices  36.9 us (19%)
  local copies, waits for them, and re-layouts  33 us (17%)
  Pallas kernels  30.9 us (16%)
  other arithmetic  24.2 us (12%)
  matrix products  16.4 us (8%)
    ppermute x6, waiting for transfers between devices, among_polar(): return lax.ppermute(block, ('lat', 'lon'), pairs)  33.7 us
    ppermute x6, starting transfers between devices, among_polar(): return lax.ppermute(block, ('lat', 'lon'), pairs)  20.8 us
    pallas_call x1, Pallas kernels, add_soundings(): pl.pallas_call(scatter_kernel, out_shape=jax.ShapeDtypeStruct((total, wid...  20.7 us
    all_to_all x1, waiting for transfers between devices, shards(): lax.all_to_all(send.reshape(devices, capacity, 32), ('lat', 'lon'), split...  16.4 us
    unnamed x60, local copies, waits for them, and re-layouts  11.4 us
    sub x3, other arithmetic, table(): full = cos_high[:, None] * cos_low[None] - sin_high[:, None] * sin_low[None]  8.38 us
    dot_general x3, matrix products, corrected(): lax.dot_general(spectra, basis, (((1,), (1,)), ((), ())), precision=preci...  8.35 us
    all_to_all x1, starting transfers between devices, shards(): lax.all_to_all(send.reshape(devices, capacity, 32), ('lat', 'lon'), split...  7.3 us
  transfers between devices with their start and end apart: 11, of which 7 were waited for; matrix products, arithmetic and copies ran while one was open for 12% of the time, Pallas kernels for 0%

profile of v3, /device:TPU:0, one launch (start us, length us, event | category | flops | bytes accessed | tf_op | source)
XLA Modules:
  0.0 196.2 jit_solution(15147016752961986318)
XLA Ops:
  6.5 5.9 %shard_map.262 = f32[8192,32]{1,0:T(8,128)S(1)} custom-call(s32[4096]{0:T(1024)S(1)} %bitcast_add_fusion.1.slots_ref, f32[4096,32]{1,0:T(8,128)S(1)} %copy.59.payload_ref), custom_call_target="tpu_custom_call" | custom-call | tf_op jit(solution)/shard_map/pallas_call | solution.py:127
  12.4 2.0 %copy-done = f32[8192,32]{1,0:T(8,128)} copy-done((f32[8192,32]{1,0:T(8,128)}, f32[8192,32]{1,0:T(8,128)S(1)}, u32[]{:S(2)}) %copy-start) | copy-done | bytes 1048600
  14.4 3.6 %copy.60 = f32[32,256,32]{1,2,0:T(8,128)} copy(f32[32,256,32]{2,1,0:T(8,128)} %bitcast.69) | data formatting | bytes 2097152 | tf_op jit(solution)/shard_map/reshape | solution.py:270
  18.0 7.3 %all-to-all-start = ((f32[32,256,32]{1,2,0:T(8,128)}), f32[32,256,32]{1,2,0:T(8,128)S(1)}, u32[]{:S(2)}, u32[]{:S(2)}) async-start(f32[32,256,32]{1,2,0:T(8,128)} %copy.60), calls=%async_computation | async-start | bytes 2097152 | tf_op jit(solution)/shard_map/all_to_all | solution.py:269
  27.4 1.7 multiply_subtract_fusion.1
  29.1 4.9 %multiply_subtract_fusion = f32[90,16,1440]{2,1,0:T(8,128)} fusion(f32[16,1440]{1,0:T(8,128)S(1)} %copy-done.15, f32[90,1440]{1,0:T(8,128)S(1)} %copy-done.9, f32[16,1440]{1,0:T(8,128)S(1)} %copy-done.14, f32[90,1440]{1,0:T(8,128)S(1)} %copy-done.8), kind=kLoop, calls=%fused_computation.4 | loop fusion | flops 6220800 | bytes 9515520 | tf_op jit(solution)/shard_map/sub | solution.py:32
  34.0 16.4 %all-to-all-done = f32[32,256,32]{1,2,0:T(8,128)S(1)} async-done(((f32[32,256,32]{1,2,0:T(8,128)}), f32[32,256,32]{1,2,0:T(8,128)S(1)}, u32[]{:S(2)}, u32[]{:S(2)}) %all-to-all-start) | async-done | bytes 1048608 | tf_op jit(solution)/shard_map/all_to_all | solution.py:269
  50.8 2.8 %copy.62.values_ref = f32[8192,48]{1,0:T(8,128)} copy(f32[8192,48]{0,1:T(8,128)S(1)} %bitcast.81) | data formatting | bytes 3145728 | tf_op jit(solution)/shard_map/mul | solution.py:277
  53.5 2.2 %copy-done.1 = f32[8192,48]{1,0:T(8,128)S(1)} copy-done((f32[8192,48]{1,0:T(8,128)S(1)}, f32[8192,48]{1,0:T(8,128)}, u32[]{:S(2)}) %copy-start.1) | copy-done | bytes 1572888
  55.7 20.7 %shard_map.263 = f32[11520,48]{1,0:T(8,128)} custom-call(s32[8192]{0:T(1024)S(1)} %bitcast.71, f32[8192,48]{1,0:T(8,128)S(1)} %copy-done.1), custom_call_target="tpu_custom_call" | custom-call | tf_op jit(solution)/shard_map/pallas_call | solution.py:141
  76.5 4.6 %copy.63 = f32[48,16,720]{2,1,0:T(8,128)S(1)} copy(f32[48,16,720]{0,2,1:T(8,128)} %bitcast.76) | data formatting | bytes 4423680 | tf_op jit(solution)/shard_map/reshape | solution.py:282
  81.2 2.2 %bitcast_add_fusion = f32[48,16,720]{2,1,0:T(8,128)S(1)} fusion(f32[48,16,720]{2,1,0:T(8,128)S(1)} %copy.63, f32[2,24,16,720]{3,2,1,0:T(8,128)} %param.28), kind=kLoop, calls=%fused_computation.6 | loop fusion | flops 552960 | bytes 6635520 | tf_op jit(solution)/shard_map/add | solution.py:281
  83.6 6.0 %collective-permute-start.1 = (f32[12,16,720]{2,1,0:T(8,128)S(1)}, f32[12,16,720]{2,1,0:T(8,128)S(1)}, u32[]{:S(2)}, u32[]{:S(2)}) collective-permute-start(f32[12,16,720]{2,1,0:T(8,128)S(1)} %get-tuple-element.40), channel_id=1, source_target_pairs={{0,3},{1,0},{2,1},{3,2},{28,31},{29,28},{30,29},{31,30}} | collective-permute-start | bytes 1658888 | tf_op jit(solution)/shard_map/ppermute | solution.py:302
  89.6 1.9 collective-permute-start.2
  91.6 3.3 %collective-permute-start = (f32[12,16,720]{2,1,0:T(8,128)S(1)}, f32[12,16,720]{2,1,0:T(8,128)S(1)}, u32[]{:S(2)}, u32[]{:S(2)}) collective-permute-start(f32[12,16,720]{2,1,0:T(8,128)S(1)} %get-tuple-element.39), channel_id=1, source_target_pairs={{0,2},{1,3},{2,0},{3,1},{28,30},{29,31},{30,28},{31,29}} | collective-permute-start | bytes 1658888 | tf_op jit(solution)/shard_map/ppermute | solution.py:302
  95.3 2.1 %collective-permute-done.1 = f32[12,16,720]{2,1,0:T(8,128)S(1)} collective-permute-done((f32[12,16,720]{2,1,0:T(8,128)S(1)}, f32[12,16,720]{2,1,0:T(8,128)S(1)}, u32[]{:S(2)}, u32[]{:S(2)}) %collective-permute-start.1) | collective-permute-done | bytes 552992 | tf_op jit(solution)/shard_map/ppermute | solution.py:302
  97.4 6.7 %collective-permute-done.2 = f32[12,16,720]{2,1,0:T(8,128)S(1)} collective-permute-done((f32[12,16,720]{2,1,0:T(8,128)S(1)}, f32[12,16,720]{2,1,0:T(8,128)S(1)}, u32[]{:S(2)}, u32[]{:S(2)}) %collective-permute-start.2) | collective-permute-done | bytes 552992 | tf_op jit(solution)/shard_map/ppermute | solution.py:302
  104.1 13.5 %collective-permute-done = f32[12,16,720]{2,1,0:T(8,128)S(1)} collective-permute-done((f32[12,16,720]{2,1,0:T(8,128)S(1)}, f32[12,16,720]{2,1,0:T(8,128)S(1)}, u32[]{:S(2)}, u32[]{:S(2)}) %collective-permute-start) | collective-permute-done | bytes 552992 | tf_op jit(solution)/shard_map/ppermute | solution.py:302
  117.8 3.9 %fusion.4 = f32[12,16,1440]{2,1,0:T(8,128)S(1)} fusion(f32[1440,1440]{1,0:T(8,128)S(1)} %bitcast.74, f32[12,16,720]{2,1,0:T(8,128)S(1)} %sub.70, f32[12,16,720]{2,1,0:T(8,128)S(1)} %sub.69, f32[16,1440]{1,0:T(8,128)S(1)} %multiply_select_fusion), kind=kOutput, calls=%fused_computation.5 | convolution fusion | flops 2389340160 | bytes 10598400 | tf_op jit(solution)/shard_map/dot_general | solution.py:53
  121.7 4.6 %fusion = f32[12,16,1440]{2,1,0:T(8,128)S(1)} fusion(f32[12,16,1440]{2,1,0:T(8,128)S(1)} %fusion.4, f32[1440,1440]{1,0:T(8,128)S(1)} %bitcast.75), kind=kOutput, calls=%fused_computation | convolution fusion | flops 2388787200 | bytes 10506240 | tf_op jit(solution)/shard_map/dot_general | solution.py:55
  130.3 2.5 %slice_subtract_fusion = (f32[12,16,720]{2,1,0:T(8,128)}, f32[12,16,720]{2,1,0:T(8,128)}, f32[12,16,720]{2,1,0:T(8,128)}, f32[48,16,720]{2,1,0:T(8,128)S(1)}) fusion(f32[12,16,1440]{2,1,0:T(8,128)S(1)} %fusion, f32[12,16,720]{2,1,0:T(8,128)S(1)} %fusion.7, f32[48,16,720]{2,1,0:T(8,128)S(1)} %copy.78, s32[]{:T(128)S(6)} %select_n.82, ...), kind=kOutput, calls=%fused_computation.31 | convolution fusion | flops 598164480 | bytes 7409668 | tf_op jit(solution)/shard_map/dot_general | solution.py:55
  132.8 1.9 collective-permute-start.3
  134.7 5.1 %collective-permute-start.4 = (f32[12,16,720]{2,1,0:T(8,128)}, f32[12,16,720]{2,1,0:T(8,128)}, u32[]{:S(2)}, u32[]{:S(2)}) collective-permute-start(f32[12,16,720]{2,1,0:T(8,128)} %get-tuple-element.50), channel_id=1, source_target_pairs={{0,2},{1,3},{2,0},{3,1},{28,30},{29,31},{30,28},{31,29}} | collective-permute-start | bytes 1658888 | tf_op jit(solution)/shard_map/ppermute | solution.py:302
  139.8 2.6 %collective-permute-start.5 = (f32[12,16,720]{2,1,0:T(8,128)}, f32[12,16,720]{2,1,0:T(8,128)}, u32[]{:S(2)}, u32[]{:S(2)}) collective-permute-start(f32[12,16,720]{2,1,0:T(8,128)} %get-tuple-element.49), channel_id=1, source_target_pairs={{0,3},{1,0},{2,1},{3,2},{28,31},{29,28},{30,29},{31,30}} | collective-permute-start | bytes 1658888 | tf_op jit(solution)/shard_map/ppermute | solution.py:302
  142.4 1.8 slice_bitcast_fusion
  148.2 11.1 %collective-permute-done.4 = f32[12,16,720]{2,1,0:T(8,128)} collective-permute-done((f32[12,16,720]{2,1,0:T(8,128)}, f32[12,16,720]{2,1,0:T(8,128)}, u32[]{:S(2)}, u32[]{:S(2)}) %collective-permute-start.4) | collective-permute-done | bytes 552992 | tf_op jit(solution)/shard_map/ppermute | solution.py:302
  166.1 1.7 pad_maximum_fusion
  167.9 2.0 %collective-permute-start.9 = (f32[3,24,720]{2,0,1:T(4,128)}, f32[3,24,720]{2,0,1:T(4,128)}, u32[]{:S(2)}, u32[]{:S(2)}) collective-permute-start(f32[3,24,720]{2,0,1:T(4,128)} %pad_maximum_fusion), channel_id=1, source_target_pairs={{0,4},{4,8},{8,12},{12,16},{16,20},{20,24},{24,28},{1,5},{5,9},{9,... | collective-permute-start | bytes 622088 | tf_op jit(solution)/shard_map/ppermute | solution.py:343
  174.1 5.6 %collective-permute-start.7 = (f32[3,24,16]{1,2,0:T(8,128)}, f32[3,24,16]{1,2,0:T(8,128)}, u32[]{:S(2)}, u32[]{:S(2)}) collective-permute-start(f32[3,24,16]{1,2,0:T(8,128)} %pad_maximum_fusion.2), channel_id=1, source_target_pairs={{0,1},{1,2},{2,3},{3,0},{4,5},{5,6},{6,7},{7,4},{8,9},{9,10},{10,1... | collective-permute-start | bytes 13832 | tf_op jit(solution)/shard_map/ppermute | solution.py:339
  179.7 1.8 copy.64
  181.5 4.0 %collective-permute-done.6 = f32[2,24,16]{1,2,0:T(8,128)S(1)} collective-permute-done((f32[2,24,16]{1,2,0:T(8,128)}, f32[2,24,16]{1,2,0:T(8,128)S(1)}, u32[]{:S(2)}, u32[]{:S(2)}) %collective-permute-start.6) | collective-permute-done | bytes 3104 | tf_op jit(solution)/shard_map/ppermute | solution.py:338
  191.9 4.3 %shard_map.264 = f32[2,24,16,720]{3,2,1,0:T(8,128)} custom-call(s32[1]{0:T(128)} %bitcast.keep_ref, f32[2,24,16,720]{3,2,1,0:T(8,128)S(1)} %bitcast.68, f32[24,16,720]{2,1,0:T(8,128)S(1)} %copy-done.2, f32[24,16,720]{2,1,0:T(8,128)S(1)} %copy-done.3, f32[24,16,5]{2,1,0:T(8,128)S(1)} %bitcast.70, f32[24,5,720]{2,1,0:T(8,128)S(1)} %maximum_bitcast_fusion.rows_ref), custom_call_target="tpu_custom_call" | custom-call | tf_op jit(solution)/shard_map/pallas_call | solution.py:209
  (104 shorter events, 34.7 us)
Async XLA Ops:
  18.0 7.5 %copy-start.24 = (s32[128]{0:T(128)S(1)}, s32[128]{0:T(128)}, u32[]{:S(2)}) copy-start(s32[128]{0:T(128)} %param.31) | copy-start | bytes 1540
  18.0 7.6 %copy-start.12 = (f32[45,720]{1,0:T(8,128)S(1)}, f32[45,720]{1,0:T(8,128)}, u32[]{:S(2)}) copy-start(f32[45,720]{1,0:T(8,128)} %constant.139.clone) | copy-start | bytes 388804
  18.0 7.6 %copy-start.13 = (f32[45,720]{1,0:T(8,128)S(1)}, f32[45,720]{1,0:T(8,128)}, u32[]{:S(2)}) copy-start(f32[45,720]{1,0:T(8,128)} %constant.140.clone) | copy-start | bytes 388804
  18.0 7.6 %copy-start.18 = (f32[16,720]{1,0:T(8,128)S(1)}, f32[16,720]{1,0:T(8,128)}, u32[]{:S(2)}) copy-start(f32[16,720]{1,0:T(8,128)} %constant.141.clone) | copy-start | bytes 138244
  18.0 7.6 %copy-start.19 = (f32[16,720]{1,0:T(8,128)S(1)}, f32[16,720]{1,0:T(8,128)}, u32[]{:S(2)}) copy-start(f32[16,720]{1,0:T(8,128)} %constant.142.clone) | copy-start | bytes 138244
  18.0 9.4 %copy-start.10 = (f32[45,720]{1,0:T(8,128)S(1)}, f32[45,720]{1,0:T(8,128)}, u32[]{:S(2)}) copy-start(f32[45,720]{1,0:T(8,128)} %constant.143.clone) | copy-start | bytes 388804
  18.0 9.3 %copy-start.11 = (f32[45,720]{1,0:T(8,128)S(1)}, f32[45,720]{1,0:T(8,128)}, u32[]{:S(2)}) copy-start(f32[45,720]{1,0:T(8,128)} %constant.144.clone) | copy-start | bytes 388804
  18.0 9.3 %copy-start.16 = (f32[16,720]{1,0:T(8,128)S(1)}, f32[16,720]{1,0:T(8,128)}, u32[]{:S(2)}) copy-start(f32[16,720]{1,0:T(8,128)} %constant.145.clone) | copy-start | bytes 138244
  18.0 9.3 %copy-start.17 = (f32[16,720]{1,0:T(8,128)S(1)}, f32[16,720]{1,0:T(8,128)}, u32[]{:S(2)}) copy-start(f32[16,720]{1,0:T(8,128)} %constant.146.clone) | copy-start | bytes 138244
  18.0 32.4 %all-to-all-start = ((f32[32,256,32]{1,2,0:T(8,128)}), f32[32,256,32]{1,2,0:T(8,128)S(1)}, u32[]{:S(2)}, u32[]{:S(2)}) async-start(f32[32,256,32]{1,2,0:T(8,128)} %copy.60), calls=%async_computation | async-start | bytes 2097152 | tf_op jit(solution)/shard_map/all_to_all | solution.py:269
  25.6 3.5 %copy-start.8 = (f32[90,1440]{1,0:T(8,128)S(1)}, f32[90,1440]{1,0:T(8,128)}, u32[]{:S(2)}) copy-start(f32[90,1440]{1,0:T(8,128)} %constant.147.clone) | copy-start | bytes 1555204
  25.6 3.5 %copy-start.9 = (f32[90,1440]{1,0:T(8,128)S(1)}, f32[90,1440]{1,0:T(8,128)}, u32[]{:S(2)}) copy-start(f32[90,1440]{1,0:T(8,128)} %constant.148.clone) | copy-start | bytes 1555204
  81.1 36.6 %slice-start = ((s8[8847360]{0:T(1024)(128)(4,1)}), s8[4194304]{0:T(1024)(128)(4,1)S(1)}, s32[]{:S(2)}) async-start(s8[8847360]{0:T(1024)(128)(4,1)} %bitcast.72), calls=%async_computation.1 | async-start | bytes 8388608
  81.1 36.6 %slice-start.1 = ((s8[8847360]{0:T(1024)(128)(4,1)}), s8[4194304]{0:T(1024)(128)(4,1)S(1)}, s32[]{:S(2)}) async-start(s8[8847360]{0:T(1024)(128)(4,1)} %bitcast.72), calls=%async_computation.2 | async-start | bytes 8388608
  83.4 11.8 %copy-start.5 = (f32[48,16,720]{2,1,0:T(8,128)}, f32[48,16,720]{2,1,0:T(8,128)S(1)}, u32[]{:S(2)}) copy-start(f32[48,16,720]{2,1,0:T(8,128)S(1)} %bitcast_add_fusion) | copy-start | bytes 6635524
  83.4 11.5 %copy-start.21 = (f32[720]{0:T(1024)S(1)}, f32[720]{0:T(1024)}, u32[]{:S(2)}) copy-start(f32[720]{0:T(1024)} %constant.153.clone) | copy-start | bytes 8644
  83.4 11.5 %copy-start.22 = (f32[720]{0:T(1024)S(1)}, f32[720]{0:T(1024)}, u32[]{:S(2)}) copy-start(f32[720]{0:T(1024)} %constant.152.clone) | copy-start | bytes 8644
  83.4 11.5 %copy-start.23 = (f32[720]{0:T(1024)S(1)}, f32[720]{0:T(1024)}, u32[]{:S(2)}) copy-start(f32[720]{0:T(1024)} %constant.151.clone) | copy-start | bytes 8644
  83.4 11.6 %copy-start.20 = (f32[1440]{0:T(1024)S(1)}, f32[1440]{0:T(1024)}, u32[]{:S(2)}) copy-start(f32[1440]{0:T(1024)} %constant.155.clone) | copy-start | bytes 17284
  83.6 13.7 %collective-permute-start.1 = (f32[12,16,720]{2,1,0:T(8,128)S(1)}, f32[12,16,720]{2,1,0:T(8,128)S(1)}, u32[]{:S(2)}, u32[]{:S(2)}) collective-permute-start(f32[12,16,720]{2,1,0:T(8,128)S(1)} %get-tuple-element.40), channel_id=1, source_target_pairs={{0,3},{1,0},{2,1},{3,2},{28,31},{29,28},{30,29},{31,30}} | collective-permute-start | bytes 1658888 | tf_op jit(solution)/shard_map/ppermute | solution.py:302
  89.6 14.4 %collective-permute-start.2 = (f32[12,16,720]{2,1,0:T(8,128)S(1)}, f32[12,16,720]{2,1,0:T(8,128)S(1)}, u32[]{:S(2)}, u32[]{:S(2)}) collective-permute-start(f32[12,16,720]{2,1,0:T(8,128)S(1)} %get-tuple-element.41), channel_id=1, source_target_pairs={{0,1},{1,2},{2,3},{3,0},{28,29},{29,30},{30,31},{31,28}} | collective-permute-start | bytes 1658888 | tf_op jit(solution)/shard_map/ppermute | solution.py:302
  91.6 26.1 %collective-permute-start = (f32[12,16,720]{2,1,0:T(8,128)S(1)}, f32[12,16,720]{2,1,0:T(8,128)S(1)}, u32[]{:S(2)}, u32[]{:S(2)}) collective-permute-start(f32[12,16,720]{2,1,0:T(8,128)S(1)} %get-tuple-element.39), channel_id=1, source_target_pairs={{0,2},{1,3},{2,0},{3,1},{28,30},{29,31},{30,28},{31,29}} | collective-permute-start | bytes 1658888 | tf_op jit(solution)/shard_map/ppermute | solution.py:302
  95.1 22.6 %slice-start.2 = ((s8[8847360]{0:T(1024)(128)(4,1)}), s8[458752]{0:T(1024)(128)(4,1)S(1)}, s32[]{:S(2)}) async-start(s8[8847360]{0:T(1024)(128)(4,1)} %bitcast.72), calls=%async_computation.3 | async-start | bytes 917504
  121.7 4.7 %copy-start.7 = (f32[45,16,720]{2,1,0:T(8,128)S(1)}, f32[45,16,720]{2,1,0:T(8,128)}, u32[]{:S(2)}) copy-start(f32[45,16,720]{2,1,0:T(8,128)} %multiply_subtract_fusion.1) | copy-start | bytes 6220804
  130.3 13.9 %copy-start.2 = (f32[24,16,720]{2,1,0:T(8,128)S(1)}, f32[24,16,720]{2,1,0:T(8,128)}, u32[]{:S(2)}) copy-start(f32[24,16,720]{2,1,0:T(8,128)} %east_ref.1) | copy-start | bytes 3317764
  132.8 14.1 %collective-permute-start.3 = (f32[12,16,720]{2,1,0:T(8,128)}, f32[12,16,720]{2,1,0:T(8,128)}, u32[]{:S(2)}, u32[]{:S(2)}) collective-permute-start(f32[12,16,720]{2,1,0:T(8,128)} %get-tuple-element.51), channel_id=1, source_target_pairs={{0,1},{1,2},{2,3},{3,0},{28,29},{29,30},{30,31},{31,28}} | collective-permute-start | bytes 1658888 | tf_op jit(solution)/shard_map/ppermute | solution.py:302
  134.7 24.6 %collective-permute-start.4 = (f32[12,16,720]{2,1,0:T(8,128)}, f32[12,16,720]{2,1,0:T(8,128)}, u32[]{:S(2)}, u32[]{:S(2)}) collective-permute-start(f32[12,16,720]{2,1,0:T(8,128)} %get-tuple-element.50), channel_id=1, source_target_pairs={{0,2},{1,3},{2,0},{3,1},{28,30},{29,31},{30,28},{31,29}} | collective-permute-start | bytes 1658888 | tf_op jit(solution)/shard_map/ppermute | solution.py:302
  139.8 20.8 %collective-permute-start.5 = (f32[12,16,720]{2,1,0:T(8,128)}, f32[12,16,720]{2,1,0:T(8,128)}, u32[]{:S(2)}, u32[]{:S(2)}) collective-permute-start(f32[12,16,720]{2,1,0:T(8,128)} %get-tuple-element.49), channel_id=1, source_target_pairs={{0,3},{1,0},{2,1},{3,2},{28,31},{29,28},{30,29},{31,30}} | collective-permute-start | bytes 1658888 | tf_op jit(solution)/shard_map/ppermute | solution.py:302
  167.9 20.7 %collective-permute-start.9 = (f32[3,24,720]{2,0,1:T(4,128)}, f32[3,24,720]{2,0,1:T(4,128)}, u32[]{:S(2)}, u32[]{:S(2)}) collective-permute-start(f32[3,24,720]{2,0,1:T(4,128)} %pad_maximum_fusion), channel_id=1, source_target_pairs={{0,4},{4,8},{8,12},{12,16},{16,20},{20,24},{24,28},{1,5},{5,9},{9,... | collective-permute-start | bytes 622088 | tf_op jit(solution)/shard_map/ppermute | solution.py:343
  171.5 17.0 %collective-permute-start.8 = (f32[2,24,720]{2,0,1:T(2,128)}, f32[2,24,720]{2,0,1:T(2,128)}, u32[]{:S(2)}, u32[]{:S(2)}) collective-permute-start(f32[2,24,720]{2,0,1:T(2,128)} %bitcast.65), channel_id=1, source_target_pairs={{4,0},{8,4},{12,8},{16,12},{20,16},{24,20},{28,24},{5,1},{9,5},{13... | collective-permute-start | bytes 414728 | tf_op jit(solution)/shard_map/ppermute | solution.py:342
  174.1 11.4 %collective-permute-start.7 = (f32[3,24,16]{1,2,0:T(8,128)}, f32[3,24,16]{1,2,0:T(8,128)}, u32[]{:S(2)}, u32[]{:S(2)}) collective-permute-start(f32[3,24,16]{1,2,0:T(8,128)} %pad_maximum_fusion.2), channel_id=1, source_target_pairs={{0,1},{1,2},{2,3},{3,0},{4,5},{5,6},{6,7},{7,4},{8,9},{9,10},{10,1... | collective-permute-start | bytes 13832 | tf_op jit(solution)/shard_map/ppermute | solution.py:339
  181.5 4.0 %collective-permute-start.6 = (f32[2,24,16]{1,2,0:T(8,128)}, f32[2,24,16]{1,2,0:T(8,128)S(1)}, u32[]{:S(2)}, u32[]{:S(2)}) collective-permute-start(f32[2,24,16]{1,2,0:T(8,128)} %bitcast.93), channel_id=1, source_target_pairs={{1,0},{2,1},{3,2},{0,3},{5,4},{6,5},{7,6},{4,7},{9,8},{10,9},{11,1... | collective-permute-start | bytes 9224 | tf_op jit(solution)/shard_map/ppermute | solution.py:338
  (7 other events, 15.0 us)

commit v4 on v3

--- a/solution.py
+++ b/solution.py
@@ -69,24 +69,20 @@
         return carry
 
     lax.fori_loop(0, total // chunk, clear, 0)
-    step = 2 * ACCS * UNROLL
+    step = 8 * UNROLL
 
     def add(i, carry):
-        base = i * step
         for turn in range(UNROLL):
-            places, news = [], []
-            for lane in range(2 * ACCS):
-                spot = base + turn * 2 * ACCS + lane
-                acc = accs[lane % ACCS]
-                place = cells_ref[spot]
-                value = values_ref[pl.ds(spot, 1), :]
-                if lane >= ACCS:
-                    same = jnp.where(place == places[lane - ACCS], 1.0, 0.0)
-                    value = value + values_ref[pl.ds(spot - ACCS, 1), :] * same
-                places.append(place)
-                news.append(acc[pl.ds(place, 1), :] + value)
-            for lane in range(2 * ACCS):
-                accs[lane % ACCS][pl.ds(places[lane], 1), :] = news[lane]
+            base = pl.multiple_of(i * step + turn * 8, 8)
+            block = values_ref[pl.ds(base, 8), :]
+            for first in range(0, 8, ACCS):
+                places = [cells_ref[base + first + lane] for lane in range(ACCS)]
+                news = [
+                    accs[lane][pl.ds(places[lane], 1), :] + block[first + lane : first + lane + 1, :]
+                    for lane in range(ACCS)
+                ]
+                for lane in range(ACCS):
+                    accs[lane][pl.ds(places[lane], 1), :] = news[lane]
         return carry
 
     lax.fori_loop(0, count // step, add, 0)
@@ -113,11 +109,11 @@
     lax.fori_loop(0, out_ref.shape[0] // chunk, clear, 0)
 
     def put(i, carry):
-        base = i * 16
-        rows = [payload_ref[pl.ds(base + j, 1), :] for j in range(16)]
+        base = pl.multiple_of(i * 16, 16)
+        block = payload_ref[pl.ds(base, 16), :]
         slots = [slots_ref[base + j] for j in range(16)]
-        for slot, row in zip(slots, rows):
-            out_ref[pl.ds(slot, 1), :] = row
+        for j, slot in enumerate(slots):
+            out_ref[pl.ds(slot, 1), :] = block[j : j + 1, :]
         return carry
 
     lax.fori_loop(0, payload_ref.shape[0] // 16, put, 0)

time: 198 us -> 197 us (level)
    ppermute x6, starting transfers between devices: 20.8 us -> 18.7 us  [among_polar(): return lax.ppermute(block, ('lat', 'lon'), pairs)]
  transfers between devices with their start and end apart: 11 -> 11, of which waited for: 7 -> 6; matrix products, arithmetic and copies ran while one was open for 12% -> 12% of each run, Pallas kernels for 0% -> 0%
where the time goes in v4:
time: 197 us; the launch traced here: 195 us
  waiting for transfers between devices  52.9 us (27%)
  starting transfers between devices  35.1 us (18%)
  local copies, waits for them, and re-layouts  33 us (17%)
  Pallas kernels  32.5 us (16%)
  other arithmetic  24.2 us (12%)
  matrix products  16.4 us (8%)
    ppermute x6, waiting for transfers between devices, among_polar(): return lax.ppermute(block, ('lat', 'lon'), pairs)  32.7 us
    pallas_call x1, Pallas kernels, add_soundings(): pl.pallas_call(scatter_kernel, out_shape=jax.ShapeDtypeStruct((total, wid...  22.3 us
    ppermute x6, starting transfers between devices, among_polar(): return lax.ppermute(block, ('lat', 'lon'), pairs)  18.7 us
    all_to_all x1, waiting for transfers between devices, shards(): lax.all_to_all(send.reshape(devices, capacity, 32), ('lat', 'lon'), split...  16.4 us
    unnamed x60, local copies, waits for them, and re-layouts  11.4 us
    sub x3, other arithmetic, table(): full = cos_high[:, None] * cos_low[None] - sin_high[:, None] * sin_low[None]  8.38 us
    dot_general x3, matrix products, corrected(): lax.dot_general(spectra, basis, (((1,), (1,)), ((), ())), precision=preci...  8.35 us
    all_to_all x1, starting transfers between devices, shards(): lax.all_to_all(send.reshape(devices, capacity, 32), ('lat', 'lon'), split...  7.3 us
  transfers between devices with their start and end apart: 11, of which 6 were waited for; matrix products, arithmetic and copies ran while one was open for 12% of the time, Pallas kernels for 0%

profile of v4, /device:TPU:0, one launch (start us, length us, event | category | flops | bytes accessed | tf_op | source)
XLA Modules:
  0.0 194.7 jit_solution(16129502598432085514)
XLA Ops:
  6.5 5.9 %shard_map.262 = f32[8192,32]{1,0:T(8,128)S(1)} custom-call(s32[4096]{0:T(1024)S(1)} %bitcast_add_fusion.1.slots_ref, f32[4096,32]{1,0:T(8,128)S(1)} %copy.59.payload_ref), custom_call_target="tpu_custom_call" | custom-call | tf_op jit(solution)/shard_map/pallas_call | solution.py:123
  12.4 2.0 %copy-done = f32[8192,32]{1,0:T(8,128)} copy-done((f32[8192,32]{1,0:T(8,128)}, f32[8192,32]{1,0:T(8,128)S(1)}, u32[]{:S(2)}) %copy-start) | copy-done | bytes 1048600
  14.4 3.6 %copy.60 = f32[32,256,32]{1,2,0:T(8,128)} copy(f32[32,256,32]{2,1,0:T(8,128)} %bitcast.69) | data formatting | bytes 2097152 | tf_op jit(solution)/shard_map/reshape | solution.py:266
  18.0 7.3 %all-to-all-start = ((f32[32,256,32]{1,2,0:T(8,128)}), f32[32,256,32]{1,2,0:T(8,128)S(1)}, u32[]{:S(2)}, u32[]{:S(2)}) async-start(f32[32,256,32]{1,2,0:T(8,128)} %copy.60), calls=%async_computation | async-start | bytes 2097152 | tf_op jit(solution)/shard_map/all_to_all | solution.py:265
  27.4 1.7 multiply_subtract_fusion.1
  29.1 4.9 %multiply_subtract_fusion = f32[90,16,1440]{2,1,0:T(8,128)} fusion(f32[16,1440]{1,0:T(8,128)S(1)} %copy-done.15, f32[90,1440]{1,0:T(8,128)S(1)} %copy-done.9, f32[16,1440]{1,0:T(8,128)S(1)} %copy-done.14, f32[90,1440]{1,0:T(8,128)S(1)} %copy-done.8), kind=kLoop, calls=%fused_computation.4 | loop fusion | flops 6220800 | bytes 9515520 | tf_op jit(solution)/shard_map/sub | solution.py:32
  34.0 16.4 %all-to-all-done = f32[32,256,32]{1,2,0:T(8,128)S(1)} async-done(((f32[32,256,32]{1,2,0:T(8,128)}), f32[32,256,32]{1,2,0:T(8,128)S(1)}, u32[]{:S(2)}, u32[]{:S(2)}) %all-to-all-start) | async-done | bytes 1048608 | tf_op jit(solution)/shard_map/all_to_all | solution.py:265
  50.8 2.8 %copy.62.values_ref = f32[8192,48]{1,0:T(8,128)} copy(f32[8192,48]{0,1:T(8,128)S(1)} %bitcast.81) | data formatting | bytes 3145728 | tf_op jit(solution)/shard_map/mul | solution.py:273
  53.5 2.2 %copy-done.1 = f32[8192,48]{1,0:T(8,128)S(1)} copy-done((f32[8192,48]{1,0:T(8,128)S(1)}, f32[8192,48]{1,0:T(8,128)}, u32[]{:S(2)}) %copy-start.1) | copy-done | bytes 1572888
  55.7 22.3 %shard_map.263 = f32[11520,48]{1,0:T(8,128)} custom-call(s32[8192]{0:T(1024)S(1)} %bitcast.71, f32[8192,48]{1,0:T(8,128)S(1)} %copy-done.1), custom_call_target="tpu_custom_call" | custom-call | tf_op jit(solution)/shard_map/pallas_call | solution.py:137
  78.0 4.6 %copy.63 = f32[48,16,720]{2,1,0:T(8,128)S(1)} copy(f32[48,16,720]{0,2,1:T(8,128)} %bitcast.76) | data formatting | bytes 4423680 | tf_op jit(solution)/shard_map/reshape | solution.py:278
  82.7 2.2 %bitcast_add_fusion = f32[48,16,720]{2,1,0:T(8,128)S(1)} fusion(f32[48,16,720]{2,1,0:T(8,128)S(1)} %copy.63, f32[2,24,16,720]{3,2,1,0:T(8,128)} %param.28), kind=kLoop, calls=%fused_computation.6 | loop fusion | flops 552960 | bytes 6635520 | tf_op jit(solution)/shard_map/add | solution.py:277
  85.1 4.0 %collective-permute-start.1 = (f32[12,16,720]{2,1,0:T(8,128)S(1)}, f32[12,16,720]{2,1,0:T(8,128)S(1)}, u32[]{:S(2)}, u32[]{:S(2)}) collective-permute-start(f32[12,16,720]{2,1,0:T(8,128)S(1)} %get-tuple-element.40), channel_id=1, source_target_pairs={{0,3},{1,0},{2,1},{3,2},{28,31},{29,28},{30,29},{31,30}} | collective-permute-start | bytes 1658888 | tf_op jit(solution)/shard_map/ppermute | solution.py:298
  89.2 2.1 %collective-permute-start.2 = (f32[12,16,720]{2,1,0:T(8,128)S(1)}, f32[12,16,720]{2,1,0:T(8,128)S(1)}, u32[]{:S(2)}, u32[]{:S(2)}) collective-permute-start(f32[12,16,720]{2,1,0:T(8,128)S(1)} %get-tuple-element.41), channel_id=1, source_target_pairs={{0,1},{1,2},{2,3},{3,0},{28,29},{29,30},{30,31},{31,28}} | collective-permute-start | bytes 1658888 | tf_op jit(solution)/shard_map/ppermute | solution.py:298
  91.3 2.6 %collective-permute-start = (f32[12,16,720]{2,1,0:T(8,128)S(1)}, f32[12,16,720]{2,1,0:T(8,128)S(1)}, u32[]{:S(2)}, u32[]{:S(2)}) collective-permute-start(f32[12,16,720]{2,1,0:T(8,128)S(1)} %get-tuple-element.39), channel_id=1, source_target_pairs={{0,2},{1,3},{2,0},{3,1},{28,30},{29,31},{30,28},{31,29}} | collective-permute-start | bytes 1658888 | tf_op jit(solution)/shard_map/ppermute | solution.py:298
  94.3 2.9 %collective-permute-done.1 = f32[12,16,720]{2,1,0:T(8,128)S(1)} collective-permute-done((f32[12,16,720]{2,1,0:T(8,128)S(1)}, f32[12,16,720]{2,1,0:T(8,128)S(1)}, u32[]{:S(2)}, u32[]{:S(2)}) %collective-permute-start.1) | collective-permute-done | bytes 552992 | tf_op jit(solution)/shard_map/ppermute | solution.py:298
  97.2 6.4 %collective-permute-done.2 = f32[12,16,720]{2,1,0:T(8,128)S(1)} collective-permute-done((f32[12,16,720]{2,1,0:T(8,128)S(1)}, f32[12,16,720]{2,1,0:T(8,128)S(1)}, u32[]{:S(2)}, u32[]{:S(2)}) %collective-permute-start.2) | collective-permute-done | bytes 552992 | tf_op jit(solution)/shard_map/ppermute | solution.py:298
  103.7 12.5 %collective-permute-done = f32[12,16,720]{2,1,0:T(8,128)S(1)} collective-permute-done((f32[12,16,720]{2,1,0:T(8,128)S(1)}, f32[12,16,720]{2,1,0:T(8,128)S(1)}, u32[]{:S(2)}, u32[]{:S(2)}) %collective-permute-start) | collective-permute-done | bytes 552992 | tf_op jit(solution)/shard_map/ppermute | solution.py:298
  116.2 3.9 %fusion.4 = f32[12,16,1440]{2,1,0:T(8,128)S(1)} fusion(f32[1440,1440]{1,0:T(8,128)S(1)} %bitcast.74, f32[12,16,720]{2,1,0:T(8,128)S(1)} %sub.70, f32[12,16,720]{2,1,0:T(8,128)S(1)} %sub.69, f32[16,1440]{1,0:T(8,128)S(1)} %multiply_select_fusion), kind=kOutput, calls=%fused_computation.5 | convolution fusion | flops 2389340160 | bytes 10598400 | tf_op jit(solution)/shard_map/dot_general | solution.py:53
  120.2 4.6 %fusion = f32[12,16,1440]{2,1,0:T(8,128)S(1)} fusion(f32[12,16,1440]{2,1,0:T(8,128)S(1)} %fusion.4, f32[1440,1440]{1,0:T(8,128)S(1)} %bitcast.75), kind=kOutput, calls=%fused_computation | convolution fusion | flops 2388787200 | bytes 10506240 | tf_op jit(solution)/shard_map/dot_general | solution.py:55
  128.8 2.5 %slice_subtract_fusion = (f32[12,16,720]{2,1,0:T(8,128)}, f32[12,16,720]{2,1,0:T(8,128)}, f32[12,16,720]{2,1,0:T(8,128)}, f32[48,16,720]{2,1,0:T(8,128)S(1)}) fusion(f32[12,16,1440]{2,1,0:T(8,128)S(1)} %fusion, f32[12,16,720]{2,1,0:T(8,128)S(1)} %fusion.7, f32[48,16,720]{2,1,0:T(8,128)S(1)} %copy.78, s32[]{:T(128)S(6)} %select_n.82, ...), kind=kOutput, calls=%fused_computation.31 | convolution fusion | flops 598164480 | bytes 7409668 | tf_op jit(solution)/shard_map/dot_general | solution.py:55
  131.3 2.8 %collective-permute-start.3 = (f32[12,16,720]{2,1,0:T(8,128)}, f32[12,16,720]{2,1,0:T(8,128)}, u32[]{:S(2)}, u32[]{:S(2)}) collective-permute-start(f32[12,16,720]{2,1,0:T(8,128)} %get-tuple-element.51), channel_id=1, source_target_pairs={{0,1},{1,2},{2,3},{3,0},{28,29},{29,30},{30,31},{31,28}} | collective-permute-start | bytes 1658888 | tf_op jit(solution)/shard_map/ppermute | solution.py:298
  134.1 5.3 %collective-permute-start.4 = (f32[12,16,720]{2,1,0:T(8,128)}, f32[12,16,720]{2,1,0:T(8,128)}, u32[]{:S(2)}, u32[]{:S(2)}) collective-permute-start(f32[12,16,720]{2,1,0:T(8,128)} %get-tuple-element.50), channel_id=1, source_target_pairs={{0,2},{1,3},{2,0},{3,1},{28,30},{29,31},{30,28},{31,29}} | collective-permute-start | bytes 1658888 | tf_op jit(solution)/shard_map/ppermute | solution.py:298
  139.3 1.9 collective-permute-start.5
  141.3 1.8 slice_bitcast_fusion
  146.8 11.0 %collective-permute-done.4 = f32[12,16,720]{2,1,0:T(8,128)} collective-permute-done((f32[12,16,720]{2,1,0:T(8,128)}, f32[12,16,720]{2,1,0:T(8,128)}, u32[]{:S(2)}, u32[]{:S(2)}) %collective-permute-start.4) | collective-permute-done | bytes 552992 | tf_op jit(solution)/shard_map/ppermute | solution.py:298
  164.6 1.7 pad_maximum_fusion
  166.3 2.0 %collective-permute-start.9 = (f32[3,24,720]{2,0,1:T(4,128)}, f32[3,24,720]{2,0,1:T(4,128)}, u32[]{:S(2)}, u32[]{:S(2)}) collective-permute-start(f32[3,24,720]{2,0,1:T(4,128)} %pad_maximum_fusion), channel_id=1, source_target_pairs={{0,4},{4,8},{8,12},{12,16},{16,20},{20,24},{24,28},{1,5},{5,9},{9,... | collective-permute-start | bytes 622088 | tf_op jit(solution)/shard_map/ppermute | solution.py:339
  172.6 5.6 %collective-permute-start.7 = (f32[3,24,16]{1,2,0:T(8,128)}, f32[3,24,16]{1,2,0:T(8,128)}, u32[]{:S(2)}, u32[]{:S(2)}) collective-permute-start(f32[3,24,16]{1,2,0:T(8,128)} %pad_maximum_fusion.2), channel_id=1, source_target_pairs={{0,1},{1,2},{2,3},{3,0},{4,5},{5,6},{6,7},{7,4},{8,9},{9,10},{10,1... | collective-permute-start | bytes 13832 | tf_op jit(solution)/shard_map/ppermute | solution.py:335
  178.2 1.8 copy.64
  180.2 3.8 %collective-permute-done.6 = f32[2,24,16]{1,2,0:T(8,128)S(1)} collective-permute-done((f32[2,24,16]{1,2,0:T(8,128)}, f32[2,24,16]{1,2,0:T(8,128)S(1)}, u32[]{:S(2)}, u32[]{:S(2)}) %collective-permute-start.6) | collective-permute-done | bytes 3104 | tf_op jit(solution)/shard_map/ppermute | solution.py:334
  190.3 4.3 %shard_map.264 = f32[2,24,16,720]{3,2,1,0:T(8,128)} custom-call(s32[1]{0:T(128)} %bitcast.keep_ref, f32[2,24,16,720]{3,2,1,0:T(8,128)S(1)} %bitcast.68, f32[24,16,720]{2,1,0:T(8,128)S(1)} %copy-done.2, f32[24,16,720]{2,1,0:T(8,128)S(1)} %copy-done.3, f32[24,16,5]{2,1,0:T(8,128)S(1)} %bitcast.70, f32[24,5,720]{2,1,0:T(8,128)S(1)} %maximum_bitcast_fusion.rows_ref), custom_call_target="tpu_custom_call" | custom-call | tf_op jit(solution)/shard_map/pallas_call | solution.py:205
  (104 shorter events, 34.6 us)
Async XLA Ops:
  18.0 7.5 %copy-start.24 = (s32[128]{0:T(128)S(1)}, s32[128]{0:T(128)}, u32[]{:S(2)}) copy-start(s32[128]{0:T(128)} %param.31) | copy-start | bytes 1540
  18.0 7.6 %copy-start.12 = (f32[45,720]{1,0:T(8,128)S(1)}, f32[45,720]{1,0:T(8,128)}, u32[]{:S(2)}) copy-start(f32[45,720]{1,0:T(8,128)} %constant.139.clone) | copy-start | bytes 388804
  18.0 7.6 %copy-start.13 = (f32[45,720]{1,0:T(8,128)S(1)}, f32[45,720]{1,0:T(8,128)}, u32[]{:S(2)}) copy-start(f32[45,720]{1,0:T(8,128)} %constant.140.clone) | copy-start | bytes 388804
  18.0 7.6 %copy-start.18 = (f32[16,720]{1,0:T(8,128)S(1)}, f32[16,720]{1,0:T(8,128)}, u32[]{:S(2)}) copy-start(f32[16,720]{1,0:T(8,128)} %constant.141.clone) | copy-start | bytes 138244
  18.0 7.6 %copy-start.19 = (f32[16,720]{1,0:T(8,128)S(1)}, f32[16,720]{1,0:T(8,128)}, u32[]{:S(2)}) copy-start(f32[16,720]{1,0:T(8,128)} %constant.142.clone) | copy-start | bytes 138244
  18.0 9.4 %copy-start.10 = (f32[45,720]{1,0:T(8,128)S(1)}, f32[45,720]{1,0:T(8,128)}, u32[]{:S(2)}) copy-start(f32[45,720]{1,0:T(8,128)} %constant.143.clone) | copy-start | bytes 388804
  18.0 9.3 %copy-start.11 = (f32[45,720]{1,0:T(8,128)S(1)}, f32[45,720]{1,0:T(8,128)}, u32[]{:S(2)}) copy-start(f32[45,720]{1,0:T(8,128)} %constant.144.clone) | copy-start | bytes 388804
  18.0 9.3 %copy-start.16 = (f32[16,720]{1,0:T(8,128)S(1)}, f32[16,720]{1,0:T(8,128)}, u32[]{:S(2)}) copy-start(f32[16,720]{1,0:T(8,128)} %constant.145.clone) | copy-start | bytes 138244
  18.0 9.3 %copy-start.17 = (f32[16,720]{1,0:T(8,128)S(1)}, f32[16,720]{1,0:T(8,128)}, u32[]{:S(2)}) copy-start(f32[16,720]{1,0:T(8,128)} %constant.146.clone) | copy-start | bytes 138244
  18.0 32.4 %all-to-all-start = ((f32[32,256,32]{1,2,0:T(8,128)}), f32[32,256,32]{1,2,0:T(8,128)S(1)}, u32[]{:S(2)}, u32[]{:S(2)}) async-start(f32[32,256,32]{1,2,0:T(8,128)} %copy.60), calls=%async_computation | async-start | bytes 2097152 | tf_op jit(solution)/shard_map/all_to_all | solution.py:265
  25.6 3.5 %copy-start.8 = (f32[90,1440]{1,0:T(8,128)S(1)}, f32[90,1440]{1,0:T(8,128)}, u32[]{:S(2)}) copy-start(f32[90,1440]{1,0:T(8,128)} %constant.147.clone) | copy-start | bytes 1555204
  25.6 3.5 %copy-start.9 = (f32[90,1440]{1,0:T(8,128)S(1)}, f32[90,1440]{1,0:T(8,128)}, u32[]{:S(2)}) copy-start(f32[90,1440]{1,0:T(8,128)} %constant.148.clone) | copy-start | bytes 1555204
  82.7 33.5 %slice-start = ((s8[8847360]{0:T(1024)(128)(4,1)}), s8[4194304]{0:T(1024)(128)(4,1)S(1)}, s32[]{:S(2)}) async-start(s8[8847360]{0:T(1024)(128)(4,1)} %bitcast.72), calls=%async_computation.1 | async-start | bytes 8388608
  82.7 33.5 %slice-start.1 = ((s8[8847360]{0:T(1024)(128)(4,1)}), s8[4194304]{0:T(1024)(128)(4,1)S(1)}, s32[]{:S(2)}) async-start(s8[8847360]{0:T(1024)(128)(4,1)} %bitcast.72), calls=%async_computation.2 | async-start | bytes 8388608
  84.9 9.3 %copy-start.5 = (f32[48,16,720]{2,1,0:T(8,128)}, f32[48,16,720]{2,1,0:T(8,128)S(1)}, u32[]{:S(2)}) copy-start(f32[48,16,720]{2,1,0:T(8,128)S(1)} %bitcast_add_fusion) | copy-start | bytes 6635524
  84.9 9.0 %copy-start.21 = (f32[720]{0:T(1024)S(1)}, f32[720]{0:T(1024)}, u32[]{:S(2)}) copy-start(f32[720]{0:T(1024)} %constant.153.clone) | copy-start | bytes 8644
  84.9 9.0 %copy-start.22 = (f32[720]{0:T(1024)S(1)}, f32[720]{0:T(1024)}, u32[]{:S(2)}) copy-start(f32[720]{0:T(1024)} %constant.152.clone) | copy-start | bytes 8644
  84.9 9.0 %copy-start.23 = (f32[720]{0:T(1024)S(1)}, f32[720]{0:T(1024)}, u32[]{:S(2)}) copy-start(f32[720]{0:T(1024)} %constant.151.clone) | copy-start | bytes 8644
  84.9 9.1 %copy-start.20 = (f32[1440]{0:T(1024)S(1)}, f32[1440]{0:T(1024)}, u32[]{:S(2)}) copy-start(f32[1440]{0:T(1024)} %constant.155.clone) | copy-start | bytes 17284
  85.1 12.1 %collective-permute-start.1 = (f32[12,16,720]{2,1,0:T(8,128)S(1)}, f32[12,16,720]{2,1,0:T(8,128)S(1)}, u32[]{:S(2)}, u32[]{:S(2)}) collective-permute-start(f32[12,16,720]{2,1,0:T(8,128)S(1)} %get-tuple-element.40), channel_id=1, source_target_pairs={{0,3},{1,0},{2,1},{3,2},{28,31},{29,28},{30,29},{31,30}} | collective-permute-start | bytes 1658888 | tf_op jit(solution)/shard_map/ppermute | solution.py:298
  89.2 14.4 %collective-permute-start.2 = (f32[12,16,720]{2,1,0:T(8,128)S(1)}, f32[12,16,720]{2,1,0:T(8,128)S(1)}, u32[]{:S(2)}, u32[]{:S(2)}) collective-permute-start(f32[12,16,720]{2,1,0:T(8,128)S(1)} %get-tuple-element.41), channel_id=1, source_target_pairs={{0,1},{1,2},{2,3},{3,0},{28,29},{29,30},{30,31},{31,28}} | collective-permute-start | bytes 1658888 | tf_op jit(solution)/shard_map/ppermute | solution.py:298
  91.3 24.9 %collective-permute-start = (f32[12,16,720]{2,1,0:T(8,128)S(1)}, f32[12,16,720]{2,1,0:T(8,128)S(1)}, u32[]{:S(2)}, u32[]{:S(2)}) collective-permute-start(f32[12,16,720]{2,1,0:T(8,128)S(1)} %get-tuple-element.39), channel_id=1, source_target_pairs={{0,2},{1,3},{2,0},{3,1},{28,30},{29,31},{30,28},{31,29}} | collective-permute-start | bytes 1658888 | tf_op jit(solution)/shard_map/ppermute | solution.py:298
  94.2 22.1 %slice-start.2 = ((s8[8847360]{0:T(1024)(128)(4,1)}), s8[458752]{0:T(1024)(128)(4,1)S(1)}, s32[]{:S(2)}) async-start(s8[8847360]{0:T(1024)(128)(4,1)} %bitcast.72), calls=%async_computation.3 | async-start | bytes 917504
  120.1 4.7 %copy-start.7 = (f32[45,16,720]{2,1,0:T(8,128)S(1)}, f32[45,16,720]{2,1,0:T(8,128)}, u32[]{:S(2)}) copy-start(f32[45,16,720]{2,1,0:T(8,128)} %multiply_subtract_fusion.1) | copy-start | bytes 6220804
  128.7 14.3 %copy-start.2 = (f32[24,16,720]{2,1,0:T(8,128)S(1)}, f32[24,16,720]{2,1,0:T(8,128)}, u32[]{:S(2)}) copy-start(f32[24,16,720]{2,1,0:T(8,128)} %east_ref.1) | copy-start | bytes 3317764
  131.3 14.2 %collective-permute-start.3 = (f32[12,16,720]{2,1,0:T(8,128)}, f32[12,16,720]{2,1,0:T(8,128)}, u32[]{:S(2)}, u32[]{:S(2)}) collective-permute-start(f32[12,16,720]{2,1,0:T(8,128)} %get-tuple-element.51), channel_id=1, source_target_pairs={{0,1},{1,2},{2,3},{3,0},{28,29},{29,30},{30,31},{31,28}} | collective-permute-start | bytes 1658888 | tf_op jit(solution)/shard_map/ppermute | solution.py:298
  134.1 23.8 %collective-permute-start.4 = (f32[12,16,720]{2,1,0:T(8,128)}, f32[12,16,720]{2,1,0:T(8,128)}, u32[]{:S(2)}, u32[]{:S(2)}) collective-permute-start(f32[12,16,720]{2,1,0:T(8,128)} %get-tuple-element.50), channel_id=1, source_target_pairs={{0,2},{1,3},{2,0},{3,1},{28,30},{29,31},{30,28},{31,29}} | collective-permute-start | bytes 1658888 | tf_op jit(solution)/shard_map/ppermute | solution.py:298
  139.3 19.8 %collective-permute-start.5 = (f32[12,16,720]{2,1,0:T(8,128)}, f32[12,16,720]{2,1,0:T(8,128)}, u32[]{:S(2)}, u32[]{:S(2)}) collective-permute-start(f32[12,16,720]{2,1,0:T(8,128)} %get-tuple-element.49), channel_id=1, source_target_pairs={{0,3},{1,0},{2,1},{3,2},{28,31},{29,28},{30,29},{31,30}} | collective-permute-start | bytes 1658888 | tf_op jit(solution)/shard_map/ppermute | solution.py:298
  166.3 20.7 %collective-permute-start.9 = (f32[3,24,720]{2,0,1:T(4,128)}, f32[3,24,720]{2,0,1:T(4,128)}, u32[]{:S(2)}, u32[]{:S(2)}) collective-permute-start(f32[3,24,720]{2,0,1:T(4,128)} %pad_maximum_fusion), channel_id=1, source_target_pairs={{0,4},{4,8},{8,12},{12,16},{16,20},{20,24},{24,28},{1,5},{5,9},{9,... | collective-permute-start | bytes 622088 | tf_op jit(solution)/shard_map/ppermute | solution.py:339
  170.0 17.0 %collective-permute-start.8 = (f32[2,24,720]{2,0,1:T(2,128)}, f32[2,24,720]{2,0,1:T(2,128)}, u32[]{:S(2)}, u32[]{:S(2)}) collective-permute-start(f32[2,24,720]{2,0,1:T(2,128)} %bitcast.65), channel_id=1, source_target_pairs={{4,0},{8,4},{12,8},{16,12},{20,16},{24,20},{28,24},{5,1},{9,5},{13... | collective-permute-start | bytes 414728 | tf_op jit(solution)/shard_map/ppermute | solution.py:338
  172.6 11.4 %collective-permute-start.7 = (f32[3,24,16]{1,2,0:T(8,128)}, f32[3,24,16]{1,2,0:T(8,128)}, u32[]{:S(2)}, u32[]{:S(2)}) collective-permute-start(f32[3,24,16]{1,2,0:T(8,128)} %pad_maximum_fusion.2), channel_id=1, source_target_pairs={{0,1},{1,2},{2,3},{3,0},{4,5},{5,6},{6,7},{7,4},{8,9},{9,10},{10,1... | collective-permute-start | bytes 13832 | tf_op jit(solution)/shard_map/ppermute | solution.py:335
  180.0 4.0 %collective-permute-start.6 = (f32[2,24,16]{1,2,0:T(8,128)}, f32[2,24,16]{1,2,0:T(8,128)S(1)}, u32[]{:S(2)}, u32[]{:S(2)}) collective-permute-start(f32[2,24,16]{1,2,0:T(8,128)} %bitcast.93), channel_id=1, source_target_pairs={{1,0},{2,1},{3,2},{0,3},{5,4},{6,5},{7,6},{4,7},{9,8},{10,9},{11,1... | collective-permute-start | bytes 9224 | tf_op jit(solution)/shard_map/ppermute | solution.py:334
  (7 other events, 15.0 us)
